TPU v7x, 128 devices: a whole 4x4x4 slice. The times are simulated.
128 devices in a mesh: gx: 8 (over y, core), gy: 16 (over z, x).
Axes of the slice: x: 4, y: 4, z: 4, core: 2. Of those that a mesh axis runs over, the one named last changes fastest.
Arguments:
- atm_tracers: float32 [16, 72, 131072], P(None, None, ('gx', 'gy')), may hold values from -4 to 6
- vert_inverse: float32 [1024, 72, 72], P(('gx', 'gy')), may hold values from 0 to 2
- ocean_tracers: float32 [16, 4, 512, 1024], P(None, None, 'gy', 'gx'), may hold values from -4 to 6
- velocity: float32 [2, 512, 1024], P(None, 'gy', 'gx'), may hold values from -0.3 to 0.3
- land_mask: int32 [512, 1024], P('gy', 'gx'), may hold values 0 or 1
- intersections: int32 [3, 9216], P(None, ('gx', 'gy')), may hold values from -1 to 63, as said below
- regrid_weights: float32 [8192, 128, 128], P(('gx', 'gy')), may hold values from 0.001 to 0.006
Outputs:
- atm_new: float32 [16, 72, 131072], P(None, None, ('gx', 'gy'))
- ocean_new: float32 [16, 4, 512, 1024], P(None, None, 'gy', 'gx')
Inputs may be any that keep to these rules, and one draw needn't show every extreme that they name: `intersections`: row 1 is -1 in empty slots, else an ocean block row below 32; row 0 is below 8 and row 2 below 64.
All inputs are finite; a program needn't handle non-finite values. No bound on the sum of `land_mask` on one device may be relied on, other than what follows from the above.
Results may differ from a plain program's by a relative error of at most 0.0003.
Values sent between devices are 32-bit elements; how exact they have to be, the bound alone decides.
A program may use at most 192 MiB of HBM per device.

v0:
```python
import jax
import jax.numpy as jnp
from jax import lax
from jax.sharding import PartitionSpec as P

K = 16
LA = 72
BLK = 128
ACB = 8
CAP = 8
NSUB = 4


ocean_uptake = 0.5
air_uptake = 0.5
mix_horizontal = 0.15
mix_vertical = 0.2


def padded_2(value, sides, width):
    for axis, dim in sides:
        devices, length = (lax.axis_size(axis), value.shape[dim])
        up = [(i, (i + 1) % devices) for i in range(devices)]
        down = [(j, i) for i, j in up]
        last = lax.slice_in_dim(value, length - width, length, axis=dim)
        leading = lax.slice_in_dim(value, 0, width, axis=dim)
        before = lax.ppermute(last, axis, up)
        after = lax.ppermute(leading, axis, down)
        value = jnp.concatenate([before, value, after], axis=dim)
    return value


def target_rows(ocean_row, contrib, tile_rows):
    highest = lax.Precision.HIGHEST
    row_onehot = (ocean_row[:, None] == jnp.arange(tile_rows, dtype=jnp.int32)[None, :]).astype(
        jnp.float32
    )
    slots = contrib.shape[0] // 9
    by_target = jnp.einsum(
        "gcr,gckb->gkrb",
        row_onehot.reshape(9, slots, tile_rows),
        contrib.reshape(9, slots, contrib.shape[1], contrib.shape[2]),
        precision=highest,
    )
    return by_target.reshape(3, 3, contrib.shape[1], tile_rows, contrib.shape[2])


def body(
    atm_tracers, vert_inverse, ocean_tracers, velocity, land_mask, intersections, regrid_weights
):
    highest = lax.Precision.HIGHEST
    slot_total = 9 * CAP
    wet_cells = land_mask.astype(jnp.float32)
    ocean_top = ocean_tracers[:, 0]
    tile_rows = ocean_top.shape[1]
    atm_surface = atm_tracers[:, 0, :]
    atm_slot = intersections[0]
    ocean_row = intersections[1]
    weight_slot = intersections[2]
    is_valid = ocean_row >= 0
    groups = jnp.arange(slot_total, dtype=jnp.int32) // CAP
    weights = regrid_weights[weight_slot]
    atm_blocks = atm_surface.reshape(K, ACB, BLK).transpose(1, 0, 2)
    own_blocks = atm_blocks[atm_slot]
    contrib = jnp.einsum("eka,eca->ekc", own_blocks, weights, precision=highest)
    by_target = target_rows(ocean_row, contrib, tile_rows)
    arrived = padded_2(by_target.reshape(1, 1, 9, K, tile_rows, BLK), (("gx", 1), ("gy", 0)), 1)
    arrived = arrived.reshape(9, 9, K, tile_rows, BLK)
    sources = jnp.arange(9, dtype=jnp.int32)
    ocean_in = jnp.sum(arrived[sources, 8 - sources], axis=0)
    surface_ext = jnp.concatenate([ocean_top * wet_cells, wet_cells[None]], 0).reshape(
        K + 1, 1, 1, tile_rows * BLK
    )
    near_tiles = padded_2(surface_ext, (("gx", 2), ("gy", 1)), 1)
    near_tiles = near_tiles.reshape(K + 1, 9 * tile_rows, BLK)
    picked = near_tiles[:, groups * tile_rows + jnp.maximum(ocean_row, 0)]
    returned = jnp.einsum("kec,eca->eka", picked, weights, precision=highest)
    atm_onehot = (
        (atm_slot[:, None] == jnp.arange(ACB, dtype=jnp.int32)[None, :]) & is_valid[:, None]
    ).astype(jnp.float32)
    atm_in = jnp.einsum("eb,eka->kba", atm_onehot, returned, precision=highest).reshape(
        K + 1, ACB * BLK
    )
    bottom = atm_surface + air_uptake * (atm_in[:K] - atm_in[K][None] * atm_surface)
    column_state = atm_tracers.at[:, 0, :].set(bottom).reshape(K, LA, ACB, BLK)
    atm_new = jnp.einsum("bij,kjbc->kibc", vert_inverse, column_state, precision=highest).reshape(
        K, LA, ACB * BLK
    )
    new_top = ocean_top + ocean_uptake * wet_cells * (ocean_in - ocean_top)
    tracer = ocean_tracers.at[:, 0].set(new_top) * wet_cells
    east_speed = velocity[0]
    north_speed = velocity[1]
    for substep in range(NSUB):
        padded = padded_2(tracer, (("gx", 3), ("gy", 2)), 1)
        east_cells = padded[:, :, 1:-1, 2:]
        west_cells = padded[:, :, 1:-1, :-2]
        north_cells = padded[:, :, 2:, 1:-1]
        south_cells = padded[:, :, :-2, 1:-1]
        tendency = -0.5 * east_speed * (east_cells - west_cells) - 0.5 * north_speed * (
            north_cells - south_cells
        )
        tendency = tendency + mix_horizontal * (
            east_cells + west_cells + north_cells + south_cells - 4.0 * tracer
        )
        above_level = jnp.concatenate([tracer[:, :1], tracer[:, :-1]], 1)
        below_level = jnp.concatenate([tracer[:, 1:], tracer[:, -1:]], 1)
        tracer = wet_cells * (
            tracer + tendency + mix_vertical * (above_level + below_level - 2.0 * tracer)
        )
    return (atm_new, tracer)


def solution(mesh):
    in_specs = (
        P(None, None, ("gx", "gy")),
        P(("gx", "gy"), None, None),
        P(None, None, "gy", "gx"),
        P(None, "gy", "gx"),
        P("gy", "gx"),
        P(None, ("gx", "gy")),
        P(("gx", "gy"), None, None),
    )
    out_specs = (P(None, None, ("gx", "gy")), P(None, None, "gy", "gx"))
    return jax.shard_map(body, mesh=mesh, in_specs=in_specs, out_specs=out_specs, check_vma=False)
```

profile of v0, /device:TPU:0, one launch (start us, length us, event | category | flops | bytes accessed | tf_op | source)
XLA Modules:
  0.0 512.1 jit_solution(2089341660246367704)
XLA Ops:
  0.7 2.4 copy.235
  3.1 2.1 copy-done.6
  6.0 5.2 %gather_fusion.1 = f32[72,128,128]{2,1,0:T(8,128)} fusion(f32[64,128,128]{2,1,0:T(8,128)} %param.17, s32[1024]{0:T(1024)S(1)} %get-tuple-element.76), kind=kCustom, calls=%fused_computation.1 | custom fusion | bytes 9437472 | tf_op jit(solution)/shard_map/gather | solution.py:62
  11.8 9.2 %fusion.62 = f32[72,16,128]{2,1,0:T(8,128)S(1)} fusion(f32[72,16,128]{2,1,0:T(8,128)S(1)} %gather_fusion.2, f32[72,128,128]{2,1,0:T(8,128)} %gather_fusion.1), kind=kOutput, calls=%fused_computation.140 | convolution fusion | flops 226492416 | bytes 5898240 | tf_op jit(solution)/shard_map/eka,eca->ekc/dot_general | solution.py:65
  22.4 2.6 collective-permute-start.5
  25.0 26.4 %collective-permute-done.5 = f32[1,1,9,16,32,128]{5,4,3,2,1,0:T(8,128)S(1)} collective-permute-done((f32[1,1,9,16,32,128]{5,4,3,2,1,0:T(8,128)S(1)}, f32[1,1,9,16,32,128]{5,4,3,2,1,0:T(8,128)S(1)}, u32[]{:S(2)}, u32[]{:S(2)}) %collective-permute-start.5) | collective-permute-done | bytes 2359328 | tf_op jit(solution)/shard_map/ppermute | solution.py:28
  51.3 3.1 collective-permute-done.4
  54.4 3.7 pad_maximum_fusion.1
  58.2 6.2 %collective-permute-start.7 = (f32[1,3,9,16,32,128]{5,4,3,2,1,0:T(8,128)}, f32[1,3,9,16,32,128]{5,4,3,2,1,0:T(8,128)}, u32[]{:S(2)}, u32[]{:S(2)}) collective-permute-start(f32[1,3,9,16,32,128]{5,4,3,2,1,0:T(8,128)} %pad_maximum_fusion.1), channel_id=1, source_target_pairs={{1,0},{2,1},{3,2},{4,3},{5,4},{6,5},{7,6},{8,7},{9,8},{10,9},{11,1... | collective-permute-start | bytes 21233672 | tf_op jit(solution)/shard_map/ppermute | solution.py:28
  66.8 3.8 copy.190
  72.1 3.1 collective-permute-done
  78.1 5.2 %collective-permute-start.3 = (f32[17,1,3,4096]{3,1,2,0:T(1,128)}, f32[17,1,3,4096]{3,1,2,0:T(1,128)}, u32[]{:S(2)}, u32[]{:S(2)}) collective-permute-start(f32[17,1,3,4096]{3,1,2,0:T(1,128)} %copy.177), channel_id=1, source_target_pairs={{1,0},{2,1},{3,2},{4,3},{5,4},{6,5},{7,6},{8,7},{9,8},{10,9},{11,1... | collective-permute-start | bytes 2506760 | tf_op jit(solution)/shard_map/ppermute | solution.py:28
  85.3 146.2 %collective-permute-done.3 = f32[17,1,3,4096]{3,1,2,0:T(1,128)} collective-permute-done((f32[17,1,3,4096]{3,1,2,0:T(1,128)}, f32[17,1,3,4096]{3,1,2,0:T(1,128)}, u32[]{:S(2)}, u32[]{:S(2)}) %collective-permute-start.3) | collective-permute-done | bytes 835616 | tf_op jit(solution)/shard_map/ppermute | solution.py:28
  233.1 3.9 collective-permute-done.2
  240.0 3.4 copy.181
  243.4 5.5 %reshape.305 = f32[17,288,128]{2,1,0:T(8,128)} reshape(f32[17,3,3,4096]{3,2,1,0:T(4,128)} %copy.181) | data formatting | bytes 5013504 | tf_op jit(solution)/shard_map/reshape | solution.py:75
  248.9 5.0 copy.182
  253.9 2.6 gather_fusion
  256.5 5.8 %fusion.22 = f32[72,17,128]{2,1,0:T(8,128)S(1)} fusion(f32[72,128,128]{2,1,0:T(8,128)} %gather_fusion.1, f32[72,17,128]{2,1,0:T(8,128)S(1)} %gather_fusion), kind=kOutput, calls=%fused_computation.72 | convolution fusion | flops 240648192 | bytes 5971968 | tf_op jit(solution)/shard_map/kec,eca->eka/dot_general | solution.py:77
  263.7 2.0 scatter.6
  265.7 6.3 %fusion.19 = f32[8,16,9,8,128]{4,3,2,1,0:T(8,128)S(1)} fusion(f32[8,72,72]{2,1,0:T(8,128)S(1)} %copy-done, f32[16,72,1024]{2,1,0:T(8,128)} %scatter.6), kind=kOutput, calls=%fused_computation.67 | convolution fusion | flops 1019215872 | bytes 9603072 | tf_op jit(solution)/shard_map/bij,kjbc->kibc/dot_general | solution.py:86
  272.0 3.1 copy.230
  276.0 13.4 %pad_maximum_fusion = f32[3,3,9,16,32,128]{5,4,3,2,1,0:T(8,128)} fusion(f32[1,3,9,16,32,128]{5,4,3,2,1,0:T(8,128)} %collective-permute-done.7, f32[1,1,9,16,32,128]{5,4,3,2,1,0:T(8,128)S(1)} %copy-done.8, f32[1,1,9,16,32,128]{5,4,3,2,1,0:T(8,128)S(1)} %convolution_bitcast_fusion, f32[1,1,9,16,32,128]{5,4,3,2,1,0:T(8,128)S(1)} %copy-done.10, ...), kind=kLoop, calls=%fused_computation.4 | loop fusion | flops 21233664 | bytes 42467328 | tf_op jit(solution)/shard_map/concatenate | solution.py:29
  289.5 7.8 %gather_fusion.3 = f32[9,16,32,128]{3,2,1,0:T(8,128)S(1)} fusion(f32[9,9,16,32,128]{4,3,2,1,0:T(8,128)} %bitcast.87, s32[9]{0:T(128)S(1)} %fusion.40), kind=kCustom, calls=%fused_computation.3 | custom fusion | bytes 4718664 | tf_op jit(solution)/shard_map/gather | solution.py:70
  300.1 2.6 broadcast_multiply_fusion
  302.7 3.4 collective-permute-start.8
  306.0 2.2 fusion.60
  308.3 2.3 collective-permute-done.9
  310.9 4.7 fusion.49
  315.7 4.5 copy.194
  321.7 4.7 copy.196
  326.9 3.0 fusion.61
  329.9 4.7 copy.195
  334.7 4.7 copy.197
  339.3 15.0 %fusion.6 = f32[16,4,32,128]{2,0,3,1:T(8,128)S(1)} fusion(f32[16,3,32,128]{2,0,3,1:T(8,128)} %get-tuple-element.63, f32[16,1,32,128]{2,0,3,1:T(8,128)} %get-tuple-element.65, f32[16,1,32,128]{2,0,3,1:T(8,128)} %get-tuple-element.64, f32[16,3,32,128]{2,0,3,1:T(8,128)S(1)} %get-tuple-element.62, f32[16,4,32,128]{2,0,3,1:T(8,128)} %copy-done.5, ...), kind=kLoop, calls=%fused_computation.50 | loop fusion | flops 7602176 | bytes 4326400 | tf_op jit(solution)/shard_map/mul | solution.py:107
  354.9 2.4 fusion.57
  359.4 4.7 fusion.48
  364.1 4.1 copy.198
  368.2 4.9 collective-permute-start.14
  373.1 4.9 copy.200
  377.9 3.0 fusion.58
  380.9 4.7 copy.199
  385.8 4.7 copy.201
  390.5 15.0 %fusion.10 = f32[16,4,32,128]{2,0,3,1:T(8,128)S(1)} fusion(f32[16,3,32,128]{2,0,3,1:T(8,128)} %get-tuple-element.57, f32[16,1,32,128]{2,0,3,1:T(8,128)} %get-tuple-element.59, f32[16,1,32,128]{2,0,3,1:T(8,128)} %get-tuple-element.58, f32[16,3,32,128]{2,0,3,1:T(8,128)S(1)} %get-tuple-element.56, f32[16,4,32,128]{2,0,3,1:T(8,128)} %copy-done.3, ...), kind=kLoop, calls=%fused_computation.55 | loop fusion | flops 7602176 | bytes 4326400 | tf_op jit(solution)/shard_map/mul | solution.py:107
  406.1 2.4 fusion.54
  410.6 4.7 fusion.47
  415.3 4.1 copy.202
  419.4 5.1 %collective-permute-start.18 = (f32[16,4,1,130]{3,0,2,1:T(8,128)S(1)}, f32[16,4,1,130]{3,0,2,1:T(8,128)}, u32[]{:S(2)}, u32[]{:S(2)}) collective-permute-start(f32[16,4,1,130]{3,0,2,1:T(8,128)S(1)} %copy.202), channel_id=1, source_target_pairs={{1,0},{2,1},{3,2},{4,3},{5,4},{6,5},{7,6},{8,7},{9,8},{10,9},{11,1... | collective-permute-start | bytes 99848 | tf_op jit(solution)/shard_map/ppermute | solution.py:28
  424.5 4.7 copy.204
  429.2 3.0 fusion.55
  432.2 4.9 copy.203
  437.1 4.7 copy.205
  441.8 15.0 %fusion.14 = f32[16,4,32,128]{2,0,3,1:T(8,128)S(1)} fusion(f32[16,3,32,128]{2,0,3,1:T(8,128)} %get-tuple-element.51, f32[16,1,32,128]{2,0,3,1:T(8,128)} %get-tuple-element.53, f32[16,1,32,128]{2,0,3,1:T(8,128)} %get-tuple-element.52, f32[16,3,32,128]{2,0,3,1:T(8,128)S(1)} %get-tuple-element.50, f32[16,4,32,128]{2,0,3,1:T(8,128)} %copy-done.4, ...), kind=kLoop, calls=%fused_computation.60 | loop fusion | flops 7602176 | bytes 4326400 | tf_op jit(solution)/shard_map/mul | solution.py:107
  457.3 2.4 fusion.51
  459.7 1.9 collective-permute-done.21
  462.3 4.7 fusion.46
  467.0 4.1 copy.206
  471.1 5.1 %collective-permute-start.22 = (f32[16,4,1,130]{3,0,2,1:T(8,128)S(1)}, f32[16,4,1,130]{3,0,2,1:T(8,128)S(1)}, u32[]{:S(2)}, u32[]{:S(2)}) collective-permute-start(f32[16,4,1,130]{3,0,2,1:T(8,128)S(1)} %copy.206), channel_id=1, source_target_pairs={{1,0},{2,1},{3,2},{4,3},{5,4},{6,5},{7,6},{8,7},{9,8},{10,9},{11,1... | collective-permute-start | bytes 99848 | tf_op jit(solution)/shard_map/ppermute | solution.py:28
  476.2 4.1 copy.208
  480.4 3.0 fusion.52
  483.4 4.2 copy.207
  487.9 3.9 copy.209
  491.9 16.2 %fusion.18 = f32[16,4,32,128]{2,0,3,1:T(8,128)} fusion(f32[16,3,32,128]{2,0,3,1:T(8,128)} %get-tuple-element.45, f32[16,1,32,128]{2,0,3,1:T(8,128)} %get-tuple-element.47, f32[16,1,32,128]{2,0,3,1:T(8,128)} %get-tuple-element.46, f32[16,3,32,128]{2,0,3,1:T(8,128)S(1)} %get-tuple-element.44, f32[16,4,32,128]{2,0,3,1:T(8,128)} %copy-done.2, ...), kind=kLoop, calls=%fused_computation.65 | loop fusion | flops 7602176 | bytes 4326400 | tf_op jit(solution)/shard_map/mul | solution.py:107
  508.1 3.6 copy.210
  (117 shorter events, 31.0 us)
Async XLA Ops:
  0.6 265.0 %copy-start = (f32[8,72,72]{2,1,0:T(8,128)S(1)}, f32[8,72,72]{2,1,0:T(8,128)}, u32[]{:S(2)}) copy-start(f32[8,72,72]{2,1,0:T(8,128)} %param.12) | copy-start | bytes 497668
  0.6 2.4 copy-start.19
  3.0 2.2 copy-start.6
  5.3 0.6 copy-start.14
  22.4 43.1 %copy-start.16 = (s32[32,128]{1,0:T(8,128)S(1)}, s32[32,128]{1,0:T(8,128)}, u32[]{:S(2)}) copy-start(s32[32,128]{1,0:T(8,128)} %param.15) | copy-start | bytes 49156
  22.4 28.9 %collective-permute-start.5 = (f32[1,1,9,16,32,128]{5,4,3,2,1,0:T(8,128)S(1)}, f32[1,1,9,16,32,128]{5,4,3,2,1,0:T(8,128)S(1)}, u32[]{:S(2)}, u32[]{:S(2)}) collective-permute-start(f32[1,1,9,16,32,128]{5,4,3,2,1,0:T(8,128)S(1)} %convolution_bitcast_fusion), channel_id=1, source_target_pairs={{16,0},{32,16},{48,32},{64,48},{80,64},{96,80},{112,96},{0,112},{1... | collective-permute-start | bytes 7077896 | tf_op jit(solution)/shard_map/ppermute | solution.py:28
  25.0 29.5 %collective-permute-start.4 = (f32[1,1,9,16,32,128]{5,4,3,2,1,0:T(8,128)S(1)}, f32[1,1,9,16,32,128]{5,4,3,2,1,0:T(8,128)S(1)}, u32[]{:S(2)}, u32[]{:S(2)}) collective-permute-start(f32[1,1,9,16,32,128]{5,4,3,2,1,0:T(8,128)S(1)} %convolution_bitcast_fusion), channel_id=1, source_target_pairs={{0,16},{16,32},{32,48},{48,64},{64,80},{80,96},{96,112},{112,0},{1... | collective-permute-start | bytes 7077896 | tf_op jit(solution)/shard_map/ppermute | solution.py:27
  51.3 6.9 %copy-start.7 = (f32[1,1,9,16,32,128]{5,4,3,2,1,0:T(8,128)}, f32[1,1,9,16,32,128]{5,4,3,2,1,0:T(8,128)S(1)}, u32[]{:S(2)}) copy-start(f32[1,1,9,16,32,128]{5,4,3,2,1,0:T(8,128)S(1)} %collective-permute-done.5) | copy-start | bytes 7077892
  54.4 3.8 copy-start.9
  58.2 216.8 %collective-permute-start.7 = (f32[1,3,9,16,32,128]{5,4,3,2,1,0:T(8,128)}, f32[1,3,9,16,32,128]{5,4,3,2,1,0:T(8,128)}, u32[]{:S(2)}, u32[]{:S(2)}) collective-permute-start(f32[1,3,9,16,32,128]{5,4,3,2,1,0:T(8,128)} %pad_maximum_fusion.1), channel_id=1, source_target_pairs={{1,0},{2,1},{3,2},{4,3},{5,4},{6,5},{7,6},{8,7},{9,8},{10,9},{11,1... | collective-permute-start | bytes 21233672 | tf_op jit(solution)/shard_map/ppermute | solution.py:28
  64.4 210.6 %collective-permute-start.6 = (f32[1,3,9,16,32,128]{5,4,3,2,1,0:T(8,128)}, f32[1,3,9,16,32,128]{5,4,3,2,1,0:T(8,128)}, u32[]{:S(2)}, u32[]{:S(2)}) collective-permute-start(f32[1,3,9,16,32,128]{5,4,3,2,1,0:T(8,128)} %pad_maximum_fusion.1), channel_id=1, source_target_pairs={{0,1},{1,2},{2,3},{3,4},{4,5},{5,6},{6,7},{7,8},{8,9},{9,10},{10,1... | collective-permute-start | bytes 21233672 | tf_op jit(solution)/shard_map/ppermute | solution.py:27
  66.3 16.9 %copy-start.18 = (f32[2,32,128]{2,1,0:T(8,128)S(1)}, f32[2,32,128]{2,1,0:T(8,128)}, u32[]{:S(2)}) copy-start(f32[2,32,128]{2,1,0:T(8,128)} %param.14) | copy-start | bytes 98308
  66.3 5.8 %collective-permute-start.1 = (f32[17,1,1,4096]{3,0,2,1:T(8,128)}, f32[17,1,1,4096]{3,0,2,1:T(8,128)S(1)}, u32[]{:S(2)}, u32[]{:S(2)}) collective-permute-start(f32[17,1,1,4096]{3,0,2,1:T(8,128)} %pad_maximum_fusion.40), channel_id=1, source_target_pairs={{16,0},{32,16},{48,32},{64,48},{80,64},{96,80},{112,96},{0,112},{1... | collective-permute-start | bytes 835592 | tf_op jit(solution)/shard_map/ppermute | solution.py:28
  66.5 8.7 %collective-permute-start = (f32[17,1,1,4096]{3,0,2,1:T(8,128)}, f32[17,1,1,4096]{3,0,2,1:T(8,128)}, u32[]{:S(2)}, u32[]{:S(2)}) collective-permute-start(f32[17,1,1,4096]{3,0,2,1:T(8,128)} %pad_maximum_fusion.40), channel_id=1, source_target_pairs={{0,16},{16,32},{32,48},{48,64},{64,80},{80,96},{96,112},{112,0},{1... | collective-permute-start | bytes 835592 | tf_op jit(solution)/shard_map/ppermute | solution.py:27
  78.1 153.4 %collective-permute-start.3 = (f32[17,1,3,4096]{3,1,2,0:T(1,128)}, f32[17,1,3,4096]{3,1,2,0:T(1,128)}, u32[]{:S(2)}, u32[]{:S(2)}) collective-permute-start(f32[17,1,3,4096]{3,1,2,0:T(1,128)} %copy.177), channel_id=1, source_target_pairs={{1,0},{2,1},{3,2},{4,3},{5,4},{6,5},{7,6},{8,7},{9,8},{10,9},{11,1... | collective-permute-start | bytes 2506760 | tf_op jit(solution)/shard_map/ppermute | solution.py:28
  83.2 153.8 %collective-permute-start.2 = (f32[17,1,3,4096]{3,1,2,0:T(1,128)}, f32[17,1,3,4096]{3,1,2,0:T(1,128)}, u32[]{:S(2)}, u32[]{:S(2)}) collective-permute-start(f32[17,1,3,4096]{3,1,2,0:T(1,128)} %copy.177), channel_id=1, source_target_pairs={{0,1},{1,2},{2,3},{3,4},{4,5},{5,6},{6,7},{7,8},{8,9},{9,10},{10,1... | collective-permute-start | bytes 2506760 | tf_op jit(solution)/shard_map/ppermute | solution.py:27
  272.0 3.1 copy-start.8
  272.0 4.1 copy-start.10
  289.5 8.0 %copy-start.17 = (f32[32,128]{1,0:T(8,128)S(1)}, f32[32,128]{1,0:T(8,128)}, u32[]{:S(2)}) copy-start(f32[32,128]{1,0:T(8,128)} %broadcast_multiply_fusion.2) | copy-start | bytes 49156
  297.2 2.8 copy-start.11
  302.6 7.9 %copy-start.5 = (f32[16,4,32,128]{2,0,3,1:T(8,128)}, f32[16,4,32,128]{2,0,3,1:T(8,128)S(1)}, u32[]{:S(2)}) copy-start(f32[16,4,32,128]{2,0,3,1:T(8,128)S(1)} %broadcast_multiply_fusion) | copy-start | bytes 3145732
  302.7 5.6 %collective-permute-start.8 = (f32[16,4,32,1]{2,0,3,1:T(8,128)S(1)}, f32[16,4,32,1]{2,0,3,1:T(8,128)S(1)}, u32[]{:S(2)}, u32[]{:S(2)}) collective-permute-start(f32[16,4,32,1]{2,0,3,1:T(8,128)S(1)} %get-tuple-element.61), channel_id=1, source_target_pairs={{16,0},{32,16},{48,32},{64,48},{80,64},{96,80},{112,96},{0,112},{1... | collective-permute-start | bytes 24584 | tf_op jit(solution)/shard_map/ppermute | solution.py:28
  306.0 4.6 collective-permute-start.9
  320.1 9.8 %collective-permute-start.10 = (f32[16,4,1,130]{3,0,2,1:T(8,128)S(1)}, f32[16,4,1,130]{3,0,2,1:T(8,128)}, u32[]{:S(2)}, u32[]{:S(2)}) collective-permute-start(f32[16,4,1,130]{3,0,2,1:T(8,128)S(1)} %copy.194), channel_id=1, source_target_pairs={{1,0},{2,1},{3,2},{4,3},{5,4},{6,5},{7,6},{8,7},{9,8},{10,9},{11,1... | collective-permute-start | bytes 99848 | tf_op jit(solution)/shard_map/ppermute | solution.py:28
  326.4 8.3 %collective-permute-start.11 = (f32[16,4,1,130]{3,0,2,1:T(8,128)}, f32[16,4,1,130]{3,0,2,1:T(8,128)}, u32[]{:S(2)}, u32[]{:S(2)}) collective-permute-start(f32[16,4,1,130]{3,0,2,1:T(8,128)} %copy.196), channel_id=1, source_target_pairs={{0,1},{1,2},{2,3},{3,4},{4,5},{5,6},{6,7},{7,8},{8,9},{9,10},{10,1... | collective-permute-start | bytes 99848 | tf_op jit(solution)/shard_map/ppermute | solution.py:27
  329.9 9.4 %copy-start.12 = (f32[32,128]{0,1:T(8,128)S(1)}, f32[32,128]{0,1:T(8,128)}, u32[]{:S(2)}) copy-start(f32[32,128]{0,1:T(8,128)} %copy.193) | copy-start | bytes 49156
  329.9 9.4 %copy-start.13 = (f32[32,128]{0,1:T(8,128)S(1)}, f32[32,128]{0,1:T(8,128)}, u32[]{:S(2)}) copy-start(f32[32,128]{0,1:T(8,128)} %copy.192) | copy-start | bytes 49156
  354.4 4.7 copy-start.3
  354.4 2.9 collective-permute-start.12
  354.5 4.6 collective-permute-start.13
  368.2 12.7 %collective-permute-start.14 = (f32[16,4,1,130]{3,0,2,1:T(8,128)S(1)}, f32[16,4,1,130]{3,0,2,1:T(8,128)}, u32[]{:S(2)}, u32[]{:S(2)}) collective-permute-start(f32[16,4,1,130]{3,0,2,1:T(8,128)S(1)} %copy.198), channel_id=1, source_target_pairs={{1,0},{2,1},{3,2},{4,3},{5,4},{6,5},{7,6},{8,7},{9,8},{10,9},{11,1... | collective-permute-start | bytes 99848 | tf_op jit(solution)/shard_map/ppermute | solution.py:28
  377.9 7.9 %collective-permute-start.15 = (f32[16,4,1,130]{3,0,2,1:T(8,128)}, f32[16,4,1,130]{3,0,2,1:T(8,128)}, u32[]{:S(2)}, u32[]{:S(2)}) collective-permute-start(f32[16,4,1,130]{3,0,2,1:T(8,128)} %copy.200), channel_id=1, source_target_pairs={{0,1},{1,2},{2,3},{3,4},{4,5},{5,6},{6,7},{7,8},{8,9},{9,10},{10,1... | collective-permute-start | bytes 99848 | tf_op jit(solution)/shard_map/ppermute | solution.py:27
  405.5 4.7 copy-start.4
  405.6 2.9 collective-permute-start.16
  405.6 4.6 collective-permute-start.17
  419.4 12.8 %collective-permute-start.18 = (f32[16,4,1,130]{3,0,2,1:T(8,128)S(1)}, f32[16,4,1,130]{3,0,2,1:T(8,128)}, u32[]{:S(2)}, u32[]{:S(2)}) collective-permute-start(f32[16,4,1,130]{3,0,2,1:T(8,128)S(1)} %copy.202), channel_id=1, source_target_pairs={{1,0},{2,1},{3,2},{4,3},{5,4},{6,5},{7,6},{8,7},{9,8},{10,9},{11,1... | collective-permute-start | bytes 99848 | tf_op jit(solution)/shard_map/ppermute | solution.py:28
  429.2 7.9 %collective-permute-start.19 = (f32[16,4,1,130]{3,0,2,1:T(8,128)}, f32[16,4,1,130]{3,0,2,1:T(8,128)}, u32[]{:S(2)}, u32[]{:S(2)}) collective-permute-start(f32[16,4,1,130]{3,0,2,1:T(8,128)} %copy.204), channel_id=1, source_target_pairs={{0,1},{1,2},{2,3},{3,4},{4,5},{5,6},{6,7},{7,8},{8,9},{9,10},{10,1... | collective-permute-start | bytes 99848 | tf_op jit(solution)/shard_map/ppermute | solution.py:27
  456.8 4.9 copy-start.2
  456.8 2.9 collective-permute-start.20
  457.1 4.6 collective-permute-start.21
  461.7 0.6 copy-start.15
  471.1 12.3 %collective-permute-start.22 = (f32[16,4,1,130]{3,0,2,1:T(8,128)S(1)}, f32[16,4,1,130]{3,0,2,1:T(8,128)S(1)}, u32[]{:S(2)}, u32[]{:S(2)}) collective-permute-start(f32[16,4,1,130]{3,0,2,1:T(8,128)S(1)} %copy.206), channel_id=1, source_target_pairs={{1,0},{2,1},{3,2},{4,3},{5,4},{6,5},{7,6},{8,7},{9,8},{10,9},{11,1... | collective-permute-start | bytes 99848 | tf_op jit(solution)/shard_map/ppermute | solution.py:28
  480.3 7.7 %collective-permute-start.23 = (f32[16,4,1,130]{3,0,2,1:T(8,128)S(1)}, f32[16,4,1,130]{3,0,2,1:T(8,128)S(1)}, u32[]{:S(2)}, u32[]{:S(2)}) collective-permute-start(f32[16,4,1,130]{3,0,2,1:T(8,128)S(1)} %copy.208), channel_id=1, source_target_pairs={{0,1},{1,2},{2,3},{3,4},{4,5},{5,6},{6,7},{7,8},{8,9},{9,10},{10,1... | collective-permute-start | bytes 99848 | tf_op jit(solution)/shard_map/ppermute | solution.py:27
  491.9 19.8 %copy-start.1 = (f32[8,72,72]{2,1,0:T(8,128)S(1)}, f32[8,72,72]{2,1,0:T(8,128)}, u32[]{:S(2)}) copy-start(f32[8,72,72]{2,1,0:T(8,128)} %param.12) | copy-start | bytes 497668
where the time goes:
time: 522 us; the launch traced here: 512 us
  waiting for transfers between devices  192 us (37%)
  local copies, waits for them, and re-layouts  171 us (33%)
  other arithmetic  88.4 us (17%)
  starting transfers between devices  36.7 us (7%)
  matrix products  23 us (4%)
    ppermute x12, waiting for transfers between devices, padded_2(): after = lax.ppermute(leading, axis, down)  173 us
    mul x4, other arithmetic, body(): wet_cells * (tracer + tendency + mix_vertical * (above_level + below_leve...  61.3 us
    slice x12, local copies, waits for them, and re-layouts, padded_2(): last = lax.slice_in_dim(value, length - width, length, axis=dim)  37.3 us
    ppermute x12, starting transfers between devices, padded_2(): after = lax.ppermute(leading, axis, down)  34.6 us
    slice x8, local copies, waits for them, and re-layouts, body(): below_level = jnp.concatenate([tracer[:, 1:], tracer[:, -1:]], 1)  21.3 us
    concatenate x8, other arithmetic, padded_2(): value = jnp.concatenate([before, value, after], axis=dim)  21 us
    ppermute x5, local copies, waits for them, and re-layouts, padded_2(): after = lax.ppermute(leading, axis, down)  20 us
    ppermute x5, local copies, waits for them, and re-layouts, padded_2(): before = lax.ppermute(last, axis, up)  19.6 us
  transfers between devices with their start and end apart: 24, of which 13 were waited for; matrix products, arithmetic and copies ran while one was open for 21% of the time, Pallas kernels for 0%

commit v1 on v0

v1 whole, which is shorter than its diff:
```python
import functools

import jax
import jax.numpy as jnp
from jax import lax
from jax.experimental import pallas as pl
from jax.experimental.pallas import tpu as pltpu
from jax.sharding import PartitionSpec as P

K = 16
LA = 72
OL = 4
OY = 32
BLK = 128
ACB = 8
CAP = 8
WSL = 64
NSUB = 4
SLOTS = 9 * CAP
HW = NSUB
EXT_ROWS = OY + 2 * HW
EXT_COLS = 2 * BLK

ocean_uptake = 0.5
air_uptake = 0.5
mix_horizontal = 0.15
mix_vertical = 0.2

F32 = jnp.float32
BF16 = jnp.bfloat16
MESH = pl.DeviceIdType.MESH
NEIGHBOURS = (0, 8, 1, 7, 2, 6, 3, 5)
REQUEST, CONTRIB, SURFACE, EARLY, LATE = range(5)
NQ = 4
EARLY_ROWS = NQ * 48 + 16
EARLY_STRIP = NQ * 16


def split2(x):
    hi = x.astype(BF16)
    return hi, (x - hi.astype(F32)).astype(BF16)


def split3(x):
    hi = x.astype(BF16)
    rest = x - hi.astype(F32)
    mid = rest.astype(BF16)
    return hi, mid, (rest - mid.astype(F32)).astype(BF16)


def dot(a, b):
    return jnp.dot(a, b, preferred_element_type=F32)


def dot_nt(a, b):
    return lax.dot_general(a, b, (((1,), (1,)), ((), ())), preferred_element_type=F32)


def exchange_kernel(
    inter, atm, oc, vel, mask, w_hbm,
    bottom, top, er_in, ec_in, es_in, lr_in, lc_in, ls_in,
    wbuf, abuf, ast, req, reqs, cbuf, cin, sbuf, sin, acc,
    er, ec, es, lr, lc, ls,
    wsem, asem, ssem, rsem,
):
    nx, ny = lax.axis_size("gx"), lax.axis_size("gy")
    i, j = lax.axis_index("gx"), lax.axis_index("gy")

    def device(g, sign):
        dy, dx = g // 3 - 1, g % 3 - 1
        return ((i + sign * dx + nx) % nx, (j + sign * dy + ny) % ny)

    def message(kind, g, src, dst, sign=1):
        return pltpu.make_async_remote_copy(
            src_ref=src, dst_ref=dst, send_sem=ssem.at[kind, g], recv_sem=rsem.at[kind, g],
            device_id=device(g, sign), device_id_type=MESH,
        )

    chunk = WSL // 8
    loads = [
        pltpu.make_async_copy(
            w_hbm.at[pl.ds(c * chunk, chunk)], wbuf.at[pl.ds(c * chunk, chunk)], wsem.at[c]
        )
        for c in range(8)
    ]
    surface_load = pltpu.make_async_copy(atm.at[:, pl.ds(0, 8), :], abuf, asem)
    surface_load.start()
    for load in loads:
        load.start()

    barrier = pltpu.get_barrier_semaphore()
    for g in NEIGHBOURS:
        pl.semaphore_signal(barrier, inc=1, device_id=device(g, 1), device_id_type=MESH)

    for e in range(SLOTS):
        req[e // CAP, pl.ds(e % CAP, 1), :] = jnp.full((1, BLK), inter[1, e], jnp.int32)
    reqs[4] = req[4]
    wet = mask[...].astype(F32)

    er[...] = jnp.zeros_like(er)
    es[...] = jnp.zeros_like(es)
    for q in range(NQ):
        for lev in range(1, OL):
            for p in range(4):
                row = q * 48 + (lev - 1) * 16 + p * 4
                er[0, row:row + HW, :] = oc[4 * q + p, lev, 0:HW, :]
                er[1, row:row + HW, :] = oc[4 * q + p, lev, OY - HW:OY, :]
    for n in range(3):
        row = NQ * 48 + n * 4
        field = vel[n] if n < 2 else wet
        er[0, row:row + HW, :] = field[0:HW]
        er[1, row:row + HW, :] = field[OY - HW:OY]
    for q in range(NQ):
        for lev in range(1, OL):
            turned = oc[4 * q:4 * q + 4, lev].reshape(BLK, BLK).T
            row = q * 16 + (lev - 1) * 4
            es[0, row:row + HW, :] = turned[0:HW]
            es[1, row:row + HW, :] = turned[BLK - HW:BLK]
    turned = jnp.concatenate([vel[0], vel[1], wet, jnp.zeros_like(wet)], 0).T
    es[0, 12:16, :] = turned[0:HW]
    es[1, 12:16, :] = turned[BLK - HW:BLK]
    for side in range(2):
        for blk in range(2):
            turned = er[side, blk * BLK:(blk + 1) * BLK, :].T
            ec[2 * side, blk * HW:(blk + 1) * HW, :] = turned[0:HW]
            ec[2 * side + 1, blk * HW:(blk + 1) * HW, :] = turned[BLK - HW:BLK]

    pl.semaphore_wait(barrier, len(NEIGHBOURS))

    requests = [message(REQUEST, g, req.at[g], reqs.at[g]) for g in NEIGHBOURS]
    for copy in requests:
        copy.start()

    sides = {1: 0, 7: 1}
    ends = {3: 0, 5: 1}
    corners = {0: 0, 2: 1, 6: 2, 8: 3}

    def halo(kind, rows, corner, strip, rows_in, corner_in, strip_in, count):
        copies = []
        for g in NEIGHBOURS:
            if g in sides:
                n = sides[g]
                copies.append(message(kind, g, rows.at[n, pl.ds(0, count)], rows_in.at[n]))
            elif g in ends:
                n = ends[g]
                copies.append(message(kind, g, strip.at[n], strip_in.at[n]))
            else:
                n = corners[g]
                copies.append(message(kind, g, corner.at[n], corner_in.at[n]))
        return copies

    early = halo(EARLY, er, ec, es, er_in, ec_in, es_in, EARLY_ROWS)
    for copy in early:
        copy.start()

    surface_load.wait()
    for b in range(ACB):
        block = abuf[:, 0, b * BLK:(b + 1) * BLK]
        hi, lo = split2(block)
        ast[b, 0:K, :] = hi
        ast[b, K:2 * K, :] = lo
    for load in loads:
        load.wait()

    def contrib_group(t, carry):
        g = (t // 2) * (1 - t % 2) + (8 - t // 2) * (t % 2)
        for s in range(CAP):
            e = g * CAP + s
            hi, lo = split2(wbuf[jnp.maximum(inter[2, e], 0)])
            a = ast[jnp.maximum(inter[0, e], 0)]
            first = dot_nt(a, hi)
            second = dot_nt(a[0:K], lo)
            cbuf[g, pl.ds(s, K, stride=CAP), :] = first[0:K] + first[K:2 * K] + second

        @pl.when(g != 4)
        def _():
            message(CONTRIB, g, cbuf.at[g], cin.at[g]).start()

        return carry

    lax.fori_loop(0, 9, contrib_group, 0)
    cin[4] = cbuf[4]

    for copy in requests:
        copy.wait_recv()
    lanes = lax.broadcasted_iota(jnp.int32, (SLOTS, BLK), 1)
    chosen = (reqs[...].reshape(SLOTS, BLK) == lanes).astype(F32)
    pick = chosen[:, 0:OY].astype(BF16)
    for k in range(0, K, 2):
        pair = jnp.concatenate([oc[k, 0] * wet, oc[k + 1, 0] * wet], 1)
        hi, mid, lo = split3(pair)
        rows = dot(pick, hi) + dot(pick, mid) + dot(pick, lo)
        for g in range(9):
            sbuf[g, k * CAP:(k + 1) * CAP, :] = rows[g * CAP:(g + 1) * CAP, 0:BLK]
            sbuf[g, (k + 1) * CAP:(k + 2) * CAP, :] = rows[g * CAP:(g + 1) * CAP, BLK:2 * BLK]
    rows = dot(pick, wet.astype(BF16))
    for g in range(9):
        sbuf[g, K * CAP:(K + 1) * CAP, :] = rows[g * CAP:(g + 1) * CAP]
    sin[4] = sbuf[4]
    for g in NEIGHBOURS:
        message(SURFACE, g, sbuf.at[g], sin.at[g], -1).start()

    place = chosen.T[0:OY].astype(BF16)
    for g in NEIGHBOURS:
        message(CONTRIB, g, cbuf.at[g], cin.at[g]).wait_recv()
    lr[...] = jnp.zeros_like(lr)
    ls[...] = jnp.zeros_like(ls)
    lc[...] = jnp.zeros_like(lc)
    for k in range(0, K, 2):
        pair = jnp.concatenate(
            [cin[:, n * CAP:(n + 1) * CAP, :].reshape(SLOTS, BLK) for n in (k, k + 1)], 1
        )
        hi, mid, lo = split3(pair)
        arrived = dot(place, hi) + dot(place, mid) + dot(place, lo)
        for n in range(2):
            old = oc[k + n, 0]
            new = old + ocean_uptake * wet * (arrived[:, n * BLK:(n + 1) * BLK] - old)
            top[k + n] = new
            lr[0, (k + n) * 4:(k + n) * 4 + 4, :] = new[0:HW]
            lr[1, (k + n) * 4:(k + n) * 4 + 4, :] = new[OY - HW:OY]
    for q in range(NQ):
        turned = top[4 * q:4 * q + 4].reshape(BLK, BLK).T
        ls[0, q * 8:q * 8 + HW, :] = turned[0:HW]
        ls[1, q * 8:q * 8 + HW, :] = turned[BLK - HW:BLK]
    for side in range(2):
        turned = lr[side].T
        lc[2 * side, 0:HW, :] = turned[0:HW]
        lc[2 * side + 1, 0:HW, :] = turned[BLK - HW:BLK]
    late = halo(LATE, lr, lc, ls, lr_in, lc_in, ls_in, 4 * K)
    for copy in late:
        copy.start()

    acc[...] = jnp.zeros_like(acc)

    def return_group(t, carry):
        t = (t + 8) % 9
        g = (t // 2) * (1 - t % 2) + (8 - t // 2) * (t % 2)

        @pl.when(g != 4)
        def _():
            message(SURFACE, g, sbuf.at[g], sin.at[g], -1).wait_recv()

        parts = []
        for s in range(CAP):
            e = g * CAP + s
            hi, lo = split2(wbuf[jnp.maximum(inter[2, e], 0)])
            ahi, alo = split2(sin[g, pl.ds(s, K, stride=CAP), :])
            wets = jnp.broadcast_to(sin[g, pl.ds(K * CAP + s, 1), :], (K, BLK)).astype(BF16)
            lhs = jnp.concatenate([ahi, alo, wets], 0)
            first = dot(lhs, hi)
            second = dot(lhs, lo)
            parts.append((
                first[0:K] + first[K:2 * K] + second[0:K],
                first[2 * K:2 * K + 8] + second[2 * K:2 * K + 8],
            ))
        for b in range(ACB):
            tracers, wets = acc[b, 0:K, :], acc[b, K:K + 8, :]
            for s in range(CAP):
                e = g * CAP + s
                here = jnp.where((inter[0, e] == b) & (inter[1, e] >= 0), 1.0, 0.0).astype(F32)
                tracers = tracers + here * parts[s][0]
                wets = wets + here * parts[s][1]
            acc[b, 0:K, :] = tracers
            acc[b, K:K + 8, :] = wets
        return carry

    lax.fori_loop(0, 9, return_group, 0)
    for b in range(ACB):
        old = abuf[:, 0, b * BLK:(b + 1) * BLK]
        bottom[:, b * BLK:(b + 1) * BLK] = old + air_uptake * (
            acc[b, 0:K, :] - acc[b, K:K + 1, :] * old
        )

    for copy in requests:
        copy.wait_send()
    for copy in early:
        copy.wait()
    for copy in late:
        copy.wait()
    for g in NEIGHBOURS:
        message(CONTRIB, g, cbuf.at[g], cin.at[g]).wait_send()
        message(SURFACE, g, sbuf.at[g], sin.at[g], -1).wait_send()


def exchange(inter, atm, oc, vel, mask, weights):
    vmem = pl.BlockSpec(memory_space=pltpu.VMEM)
    shapes = [
        (K, ACB * BLK), (K, OY, BLK),
        (2, EARLY_ROWS, BLK), (4, 8, BLK), (2, EARLY_STRIP, BLK),
        (2, 4 * K, BLK), (4, 8, BLK), (2, 8 * NQ, BLK),
    ]
    return pl.pallas_call(
        exchange_kernel,
        out_shape=[jax.ShapeDtypeStruct(s, F32) for s in shapes],
        in_specs=[
            pl.BlockSpec(memory_space=pltpu.SMEM),
            pl.BlockSpec(memory_space=pl.ANY),
            vmem, vmem, vmem,
            pl.BlockSpec(memory_space=pl.ANY),
        ],
        out_specs=[vmem] * len(shapes),
        scratch_shapes=[
            pltpu.VMEM((WSL, BLK, BLK), F32),
            pltpu.VMEM((K, 8, ACB * BLK), F32),
            pltpu.VMEM((ACB, 2 * K, BLK), BF16),
            pltpu.VMEM((9, CAP, BLK), jnp.int32),
            pltpu.VMEM((9, CAP, BLK), jnp.int32),
            pltpu.VMEM((9, K * CAP, BLK), F32),
            pltpu.VMEM((9, K * CAP, BLK), F32),
            pltpu.VMEM((9, (K + 1) * CAP, BLK), F32),
            pltpu.VMEM((9, (K + 1) * CAP, BLK), F32),
            pltpu.VMEM((ACB, K + 8, BLK), F32),
            pltpu.VMEM((2, 2 * BLK, BLK), F32),
            pltpu.VMEM((4, 8, BLK), F32),
            pltpu.VMEM((2, EARLY_STRIP, BLK), F32),
            pltpu.VMEM((2, BLK, BLK), F32),
            pltpu.VMEM((4, 8, BLK), F32),
            pltpu.VMEM((2, 8 * NQ, BLK), F32),
            pltpu.SemaphoreType.DMA((8,)),
            pltpu.SemaphoreType.DMA,
            pltpu.SemaphoreType.DMA((5, 9)),
            pltpu.SemaphoreType.DMA((5, 9)),
        ],
        compiler_params=pltpu.CompilerParams(collective_id=0, has_side_effects=True),
        name="exchange",
    )(inter, atm, oc, vel, mask, weights)


def step_kernel(
    atm, mix, bottom, oc, top, vel, mask, er, ec, es, lr, lc, ls,
    atm_out, oc_out, coef, xs, ct,
):
    q = pl.program_id(0)

    def spread(east, west):
        gap = jnp.zeros((BLK - 2 * HW, BLK), F32)
        return jnp.concatenate([east, gap, west], 0).T

    @pl.when(q == 0)
    def _():
        for side in range(2):
            for blk in range(2):
                ct[side, blk * BLK:(blk + 1) * BLK, :] = spread(
                    ec[2 * side, blk * HW:(blk + 1) * HW, :],
                    ec[2 * side + 1, blk * HW:(blk + 1) * HW, :],
                )
            ct[side, 2 * BLK:3 * BLK, :] = spread(lc[2 * side, 0:HW, :], lc[2 * side + 1, 0:HW, :])
        ends = spread(es[0, 12:16, :], es[1, 12:16, :])
        fields = []
        for n in range(3):
            own = vel[n] if n < 2 else mask[...].astype(F32)
            row = NQ * 48 + n * 4
            left = jnp.concatenate([own, er[0, row:row + HW, :], er[1, row:row + HW, :]], 0)
            right = jnp.concatenate(
                [ends[n * OY:(n + 1) * OY], ct[0, row:row + HW, :], ct[1, row:row + HW, :]], 0
            )
            fields.append(jnp.concatenate([left, right], 1))
        u, v, wet = fields
        coef[0] = wet * (mix_horizontal - 0.5 * u)
        coef[1] = wet * (mix_horizontal + 0.5 * u)
        coef[2] = wet * (mix_horizontal - 0.5 * v)
        coef[3] = wet * (mix_horizontal + 0.5 * v)
        coef[4] = wet * mix_vertical
        coef[5] = wet * (1.0 - 4.0 * mix_horizontal - 2.0 * mix_vertical)
        coef[6] = wet

    for lev in range(OL):
        if lev == 0:
            base = pl.multiple_of(q * 16, 16)
            north, south = lr[0, pl.ds(base, 16), :], lr[1, pl.ds(base, 16), :]
            corner = pl.multiple_of(2 * BLK + q * 16, 16)
            group = pl.multiple_of(q * 8, 8)
            ends = spread(ls[0, pl.ds(group, 8), :][0:HW], ls[1, pl.ds(group, 8), :][0:HW])
        else:
            base = pl.multiple_of(q * 48 + (lev - 1) * 16, 16)
            north, south = er[0, pl.ds(base, 16), :], er[1, pl.ds(base, 16), :]
            corner = base
            group = pl.multiple_of(q * 16, 16)
            piece = slice((lev - 1) * HW, lev * HW)
            ends = spread(es[0, pl.ds(group, 16), :][piece], es[1, pl.ds(group, 16), :][piece])
        north_ends, south_ends = ct[0, pl.ds(corner, 16), :], ct[1, pl.ds(corner, 16), :]
        for p in range(4):
            part = slice(p * 4, p * 4 + 4)
            xs[p, lev, 0:OY, 0:BLK] = top[p] if lev == 0 else oc[p, lev]
            xs[p, lev, OY:OY + HW, 0:BLK] = north[part]
            xs[p, lev, OY + HW:EXT_ROWS, 0:BLK] = south[part]
            xs[p, lev, 0:OY, BLK:EXT_COLS] = ends[p * OY:(p + 1) * OY]
            xs[p, lev, OY:OY + HW, BLK:EXT_COLS] = north_ends[part]
            xs[p, lev, OY + HW:EXT_ROWS, BLK:EXT_COLS] = south_ends[part]

    def ocean(p, carry):
        levels = [xs[p, lev] * coef[6] for lev in range(OL)]
        for _ in range(NSUB):
            new = []
            for lev in range(OL):
                x = levels[lev]
                above, below = levels[max(lev - 1, 0)], levels[min(lev + 1, OL - 1)]
                new.append(
                    coef[0] * pltpu.roll(x, EXT_COLS - 1, 1)
                    + coef[1] * pltpu.roll(x, 1, 1)
                    + coef[2] * pltpu.roll(x, EXT_ROWS - 1, 0)
                    + coef[3] * pltpu.roll(x, 1, 0)
                    + coef[4] * (above + below)
                    + coef[5] * x
                )
            levels = new
        for lev in range(OL):
            oc_out[p, lev] = levels[lev][0:OY, 0:BLK]
        return carry

    lax.fori_loop(0, 4, ocean, 0)

    for b in range(2):
        m = jnp.concatenate([mix[b], jnp.zeros((LA, EXT_COLS - LA), F32)], 1)
        mh = m.astype(BF16).astype(F32)
        stacked = (mh + pltpu.roll(mh, 80, 1) + pltpu.roll(m - mh, 160, 1)).astype(BF16)
        first = lax.broadcasted_iota(jnp.int32, (8, BLK), 0) == 0
        cols = slice(b * BLK, (b + 1) * BLK)

        for k in range(0, K, 2):
            sides = []
            for n in (k, k + 1):
                surface = jnp.broadcast_to(bottom[n:n + 1, cols], (8, BLK))
                low = jnp.where(first, surface, atm[n, 0:8, cols])
                x = jnp.concatenate([low, atm[n, 8:LA, cols], jnp.zeros((8, BLK), F32)], 0)
                hi, lo = split2(x)
                sides.append(jnp.concatenate([hi, lo, hi, jnp.zeros((16, BLK), BF16)], 0))
            out = dot(stacked, jnp.concatenate(sides, 1))
            atm_out[k, :, cols] = out[:, 0:BLK]
            atm_out[k + 1, :, cols] = out[:, BLK:2 * BLK]


def local_step(atm, mix, bottom, oc, top, vel, mask, halos):
    vmem = pl.BlockSpec(memory_space=pltpu.VMEM)
    return pl.pallas_call(
        step_kernel,
        grid=(NQ,),
        out_shape=[
            jax.ShapeDtypeStruct(atm.shape, F32),
            jax.ShapeDtypeStruct(oc.shape, F32),
        ],
        in_specs=[
            pl.BlockSpec((K, LA, 2 * BLK), lambda q: (0, 0, q)),
            pl.BlockSpec((2, LA, LA), lambda q: (q, 0, 0)),
            pl.BlockSpec((K, 2 * BLK), lambda q: (0, q)),
            pl.BlockSpec((4, OL, OY, BLK), lambda q: (q, 0, 0, 0)),
            pl.BlockSpec((4, OY, BLK), lambda q: (q, 0, 0)),
        ] + [vmem] * 8,
        out_specs=[
            pl.BlockSpec((K, LA, 2 * BLK), lambda q: (0, 0, q)),
            pl.BlockSpec((4, OL, OY, BLK), lambda q: (q, 0, 0, 0)),
        ],
        scratch_shapes=[
            pltpu.VMEM((7, EXT_ROWS, EXT_COLS), F32),
            pltpu.VMEM((4, OL, EXT_ROWS, EXT_COLS), F32),
            pltpu.VMEM((2, 3 * BLK, BLK), F32),
        ],
        name="step",
    )(atm, mix, bottom, oc, top, vel, mask, *halos)


def body(atm, mix, oc, vel, mask, inter, weights):
    bottom, top, *halos = exchange(inter, atm, oc, vel, mask, weights)
    return tuple(local_step(atm, mix, bottom, oc, top, vel, mask, halos))


def solution(mesh):
    in_specs = (
        P(None, None, ("gx", "gy")),
        P(("gx", "gy"), None, None),
        P(None, None, "gy", "gx"),
        P(None, "gy", "gx"),
        P("gy", "gx"),
        P(None, ("gx", "gy")),
        P(("gx", "gy"), None, None),
    )
    out_specs = (P(None, None, ("gx", "gy")), P(None, None, "gy", "gx"))
    return jax.shard_map(body, mesh=mesh, in_specs=in_specs, out_specs=out_specs, check_vma=False)
```

time: 522 us -> 43.2 us (0.08)
  the two profiles are of different devices: /device:TPU:0 before, /device:TPU:1 now
where the time goes in v1:
time: 43.2 us; the launch traced here: 43 us
  Pallas kernels  42.4 us (98%)
  between operations  0.64 us (1%)
    pallas_call x1, Pallas kernels, exchange(): pl.pallas_call(exchange_kernel, out_shape=[jax.ShapeDtypeStruct(s, F32) f...  29.3 us
    pallas_call x1, Pallas kernels, local_step(): pl.pallas_call(step_kernel, grid=(NQ,), out_shape=[jax.ShapeDtypeStruct(a...  13.1 us

profile of v1, /device:TPU:1, one launch (start us, length us, event | category | flops | bytes accessed | tf_op | source)
XLA Modules:
  0.0 43.0 jit_solution(14612869365460898178)
XLA Ops:
  0.6 29.3 %exchange.1 = (f32[16,1024]{1,0:T(8,128)}, f32[16,32,128]{2,1,0:T(8,128)}, f32[2,208,128]{2,1,0:T(8,128)}, f32[4,8,128]{2,1,0:T(8,128)}, f32[2,64,128]{2,1,0:T(8...) custom-call(s32[3,72]{1,0:T(4,128)} %inter.1, f32[16,72,1024]{2,1,0:T(8,128)} %atm.3, ...), custom_call_target="tpu_custom_call" | custom-call | tf_op jit(solution)/shard_map/exchange/pallas_call | solution.py:292
  30.0 13.1 %step.1 = (f32[16,72,1024]{2,1,0:T(8,128)}, f32[16,4,32,128]{3,2,1,0:T(8,128)}) custom-call(f32[16,72,1024]{2,1,0:T(8,128)} %atm.3, f32[8,72,72]{2,1,0:T(8,128)} %mix.1, f32[16,1024]{1,0:T(8,128)} %get-tuple-element.10.bottom, f32[16,4,32,128]{3,2,1,0:T(8,128)} %oc.3, f32[16,32,128]{2,1,0:T(8,128)} %get-tuple-element.11.top, f32[2,32,128]{2,1,0:T(8,128)} %vel.3, ...), custom_call_target="tpu_custom_call" | custom-call | tf_op jit(solution)/shard_map/step/pallas_call | solution.py:435

commit v2 on v1

--- a/solution.py
+++ b/solution.py
@@ -57,11 +57,11 @@
 
 
 def exchange_kernel(
-    inter, atm, oc, vel, mask, w_hbm,
-    bottom, top, er_in, ec_in, es_in, lr_in, lc_in, ls_in,
-    wbuf, abuf, ast, req, reqs, cbuf, cin, sbuf, sin, acc,
+    inter_hbm, atm_hbm, mix_hbm, oc_hbm, vel_hbm, mask_hbm, w_hbm,
+    mixed, first_column, bottom, oc, fields, er_in, ec_in, es_in, lr_in, lc_in, ls_in,
+    inter, wbuf, abuf, xbuf, mbuf, maskbuf, stacked, ast, req, reqs, cbuf, cin, sbuf, sin, acc,
     er, ec, es, lr, lc, ls,
-    wsem, asem, ssem, rsem,
+    wsem, xsem, lsem, ssem, rsem,
 ):
     nx, ny = lax.axis_size("gx"), lax.axis_size("gy")
     i, j = lax.axis_index("gx"), lax.axis_index("gy")
@@ -76,28 +76,42 @@
             device_id=device(g, sign), device_id_type=MESH,
         )
 
+    barrier = pltpu.get_barrier_semaphore()
+    for g in NEIGHBOURS:
+        pl.semaphore_signal(barrier, inc=1, device_id=device(g, 1), device_id_type=MESH)
+
     chunk = WSL // 8
+    small = [
+        pltpu.make_async_copy(src, dst, lsem.at[n])
+        for n, (src, dst) in enumerate((
+            (oc_hbm, oc), (vel_hbm, fields.at[pl.ds(0, 2)]), (mask_hbm, maskbuf),
+            (atm_hbm.at[:, pl.ds(0, 8), :], abuf), (mix_hbm, mbuf), (inter_hbm, inter),
+        ))
+    ]
     loads = [
         pltpu.make_async_copy(
             w_hbm.at[pl.ds(c * chunk, chunk)], wbuf.at[pl.ds(c * chunk, chunk)], wsem.at[c]
         )
         for c in range(8)
     ]
-    surface_load = pltpu.make_async_copy(atm.at[:, pl.ds(0, 8), :], abuf, asem)
-    surface_load.start()
-    for load in loads:
+    columns = [
+        pltpu.make_async_copy(atm_hbm.at[pl.ds(2 * c, 2)], xbuf.at[pl.ds(2 * c, 2)], xsem.at[c])
+        for c in range(8)
+    ]
+    for load in small[5:6] + small[0:5] + loads:
         load.start()
 
-    barrier = pltpu.get_barrier_semaphore()
-    for g in NEIGHBOURS:
-        pl.semaphore_signal(barrier, inc=1, device_id=device(g, 1), device_id_type=MESH)
-
+    small[5].wait()
     for e in range(SLOTS):
         req[e // CAP, pl.ds(e % CAP, 1), :] = jnp.full((1, BLK), inter[1, e], jnp.int32)
     reqs[4] = req[4]
-    wet = mask[...].astype(F32)
-
-    er[...] = jnp.zeros_like(er)
+    for load in small[0:3]:
+        load.wait()
+    wet = maskbuf[...].astype(F32)
+    fields[2] = wet
+    vel = fields
+
+    er[:, NQ * 48:2 * BLK, :] = jnp.zeros((2, 2 * BLK - NQ * 48, BLK), F32)
     es[...] = jnp.zeros_like(es)
     for q in range(NQ):
         for lev in range(1, OL):
@@ -153,7 +167,7 @@
     for copy in early:
         copy.start()
 
-    surface_load.wait()
+    small[3].wait()
     for b in range(ACB):
         block = abuf[:, 0, b * BLK:(b + 1) * BLK]
         hi, lo = split2(block)
@@ -161,6 +175,8 @@
         ast[b, K:2 * K, :] = lo
     for load in loads:
         load.wait()
+    for load in columns:
+        load.start()
 
     def contrib_group(t, carry):
         g = (t // 2) * (1 - t % 2) + (8 - t // 2) * (t % 2)
@@ -200,6 +216,36 @@
     for g in NEIGHBOURS:
         message(SURFACE, g, sbuf.at[g], sin.at[g], -1).start()
 
+    small[4].wait()
+    for b in range(ACB):
+        m = jnp.concatenate([mbuf[b], jnp.zeros((LA, 2 * BLK - LA), F32)], 1)
+        first_column[b] = jnp.broadcast_to(m[:, 0:1], (LA, BLK))
+        mh = m.astype(BF16).astype(F32)
+        stacked[b] = (mh + pltpu.roll(mh, 80, 1) + pltpu.roll(m - mh, 160, 1)).astype(BF16)
+    upper = lax.broadcasted_iota(jnp.int32, (8, BLK), 0) > 0
+
+    for c in range(8):
+        columns[c].wait()
+
+    def mixing(c, carry):
+        for b in range(ACB):
+            cols = slice(b * BLK, (b + 1) * BLK)
+            sides = []
+            for n in range(2):
+                x = jnp.concatenate([
+                    jnp.where(upper, xbuf[2 * c + n, 0:8, cols], 0.0),
+                    xbuf[2 * c + n, 8:LA, cols],
+                    jnp.zeros((8, BLK), F32),
+                ], 0)
+                hi, lo = split2(x)
+                sides.append(jnp.concatenate([hi, lo, hi, jnp.zeros((16, BLK), BF16)], 0))
+            out = dot(stacked[b], jnp.concatenate(sides, 1))
+            mixed[2 * c, :, cols] = out[:, 0:BLK]
+            mixed[2 * c + 1, :, cols] = out[:, BLK:2 * BLK]
+        return carry
+
+    lax.fori_loop(0, 8, mixing, 0)
+
     place = chosen.T[0:OY].astype(BF16)
     for g in NEIGHBOURS:
         message(CONTRIB, g, cbuf.at[g], cin.at[g]).wait_recv()
@@ -215,11 +261,11 @@
         for n in range(2):
             old = oc[k + n, 0]
             new = old + ocean_uptake * wet * (arrived[:, n * BLK:(n + 1) * BLK] - old)
-            top[k + n] = new
+            oc[k + n, 0] = new
             lr[0, (k + n) * 4:(k + n) * 4 + 4, :] = new[0:HW]
             lr[1, (k + n) * 4:(k + n) * 4 + 4, :] = new[OY - HW:OY]
     for q in range(NQ):
-        turned = top[4 * q:4 * q + 4].reshape(BLK, BLK).T
+        turned = oc[4 * q:4 * q + 4, 0].reshape(BLK, BLK).T
         ls[0, q * 8:q * 8 + HW, :] = turned[0:HW]
         ls[1, q * 8:q * 8 + HW, :] = turned[BLK - HW:BLK]
     for side in range(2):
@@ -267,7 +313,7 @@
     lax.fori_loop(0, 9, return_group, 0)
     for b in range(ACB):
         old = abuf[:, 0, b * BLK:(b + 1) * BLK]
-        bottom[:, b * BLK:(b + 1) * BLK] = old + air_uptake * (
+        bottom[pl.ds(b, K, stride=ACB), :] = old + air_uptake * (
             acc[b, 0:K, :] - acc[b, K:K + 1, :] * old
         )
 
@@ -282,26 +328,27 @@
         message(SURFACE, g, sbuf.at[g], sin.at[g], -1).wait_send()
 
 
-def exchange(inter, atm, oc, vel, mask, weights):
+def exchange(inter, atm, mix, oc, vel, mask, weights):
     vmem = pl.BlockSpec(memory_space=pltpu.VMEM)
+    hbm = pl.BlockSpec(memory_space=pltpu.HBM)
     shapes = [
-        (K, ACB * BLK), (K, OY, BLK),
+        (K, LA, ACB * BLK), (ACB, LA, BLK), (K * ACB, BLK), (K, OL, OY, BLK), (3, OY, BLK),
         (2, EARLY_ROWS, BLK), (4, 8, BLK), (2, EARLY_STRIP, BLK),
         (2, 4 * K, BLK), (4, 8, BLK), (2, 8 * NQ, BLK),
     ]
     return pl.pallas_call(
         exchange_kernel,
         out_shape=[jax.ShapeDtypeStruct(s, F32) for s in shapes],
-        in_specs=[
-            pl.BlockSpec(memory_space=pltpu.SMEM),
-            pl.BlockSpec(memory_space=pl.ANY),
-            vmem, vmem, vmem,
-            pl.BlockSpec(memory_space=pl.ANY),
-        ],
+        in_specs=[hbm] * 7,
         out_specs=[vmem] * len(shapes),
         scratch_shapes=[
+            pltpu.SMEM((3, SLOTS), jnp.int32),
             pltpu.VMEM((WSL, BLK, BLK), F32),
             pltpu.VMEM((K, 8, ACB * BLK), F32),
+            pltpu.VMEM((K, LA, ACB * BLK), F32),
+            pltpu.VMEM((ACB, LA, LA), F32),
+            pltpu.VMEM((OY, BLK), jnp.int32),
+            pltpu.VMEM((ACB, LA, 2 * BLK), BF16),
             pltpu.VMEM((ACB, 2 * K, BLK), BF16),
             pltpu.VMEM((9, CAP, BLK), jnp.int32),
             pltpu.VMEM((9, CAP, BLK), jnp.int32),
@@ -317,17 +364,23 @@
             pltpu.VMEM((4, 8, BLK), F32),
             pltpu.VMEM((2, 8 * NQ, BLK), F32),
             pltpu.SemaphoreType.DMA((8,)),
-            pltpu.SemaphoreType.DMA,
+            pltpu.SemaphoreType.DMA((8,)),
+            pltpu.SemaphoreType.DMA((6,)),
             pltpu.SemaphoreType.DMA((5, 9)),
             pltpu.SemaphoreType.DMA((5, 9)),
         ],
-        compiler_params=pltpu.CompilerParams(collective_id=0, has_side_effects=True),
+        compiler_params=pltpu.CompilerParams(
+            collective_id=0, has_side_effects=True, vmem_limit_bytes=30 * 2**20
+        ),
         name="exchange",
-    )(inter, atm, oc, vel, mask, weights)
+    )(*(
+        pltpu.with_memory_space_constraint(x, pltpu.HBM)
+        for x in (inter, atm, mix, oc, vel, mask, weights)
+    ))
 
 
 def step_kernel(
-    atm, mix, bottom, oc, top, vel, mask, er, ec, es, lr, lc, ls,
+    mixed, first_column, bottom, oc, own, er, ec, es, lr, lc, ls,
     atm_out, oc_out, coef, xs, ct,
 ):
     q = pl.program_id(0)
@@ -348,9 +401,8 @@
         ends = spread(es[0, 12:16, :], es[1, 12:16, :])
         fields = []
         for n in range(3):
-            own = vel[n] if n < 2 else mask[...].astype(F32)
             row = NQ * 48 + n * 4
-            left = jnp.concatenate([own, er[0, row:row + HW, :], er[1, row:row + HW, :]], 0)
+            left = jnp.concatenate([own[n], er[0, row:row + HW, :], er[1, row:row + HW, :]], 0)
             right = jnp.concatenate(
                 [ends[n * OY:(n + 1) * OY], ct[0, row:row + HW, :], ct[1, row:row + HW, :]], 0
             )
@@ -381,7 +433,7 @@
         north_ends, south_ends = ct[0, pl.ds(corner, 16), :], ct[1, pl.ds(corner, 16), :]
         for p in range(4):
             part = slice(p * 4, p * 4 + 4)
-            xs[p, lev, 0:OY, 0:BLK] = top[p] if lev == 0 else oc[p, lev]
+            xs[p, lev, 0:OY, 0:BLK] = oc[4 * q + p, lev]
             xs[p, lev, OY:OY + HW, 0:BLK] = north[part]
             xs[p, lev, OY + HW:EXT_ROWS, 0:BLK] = south[part]
             xs[p, lev, 0:OY, BLK:EXT_COLS] = ends[p * OY:(p + 1) * OY]
@@ -410,44 +462,26 @@
 
     lax.fori_loop(0, 4, ocean, 0)
 
-    for b in range(2):
-        m = jnp.concatenate([mix[b], jnp.zeros((LA, EXT_COLS - LA), F32)], 1)
-        mh = m.astype(BF16).astype(F32)
-        stacked = (mh + pltpu.roll(mh, 80, 1) + pltpu.roll(m - mh, 160, 1)).astype(BF16)
-        first = lax.broadcasted_iota(jnp.int32, (8, BLK), 0) == 0
-        cols = slice(b * BLK, (b + 1) * BLK)
-
-        for k in range(0, K, 2):
-            sides = []
-            for n in (k, k + 1):
-                surface = jnp.broadcast_to(bottom[n:n + 1, cols], (8, BLK))
-                low = jnp.where(first, surface, atm[n, 0:8, cols])
-                x = jnp.concatenate([low, atm[n, 8:LA, cols], jnp.zeros((8, BLK), F32)], 0)
-                hi, lo = split2(x)
-                sides.append(jnp.concatenate([hi, lo, hi, jnp.zeros((16, BLK), BF16)], 0))
-            out = dot(stacked, jnp.concatenate(sides, 1))
-            atm_out[k, :, cols] = out[:, 0:BLK]
-            atm_out[k + 1, :, cols] = out[:, BLK:2 * BLK]
-
-
-def local_step(atm, mix, bottom, oc, top, vel, mask, halos):
+    for p in range(4):
+        k = 4 * q + p
+        surface = bottom[pl.ds(pl.multiple_of(k * ACB, ACB), ACB), :]
+        for b in range(ACB):
+            cols = slice(b * BLK, (b + 1) * BLK)
+            atm_out[p, :, cols] = mixed[k, :, cols] + first_column[b] * surface[b:b + 1]
+
+
+def local_step(arrays):
     vmem = pl.BlockSpec(memory_space=pltpu.VMEM)
     return pl.pallas_call(
         step_kernel,
         grid=(NQ,),
         out_shape=[
-            jax.ShapeDtypeStruct(atm.shape, F32),
-            jax.ShapeDtypeStruct(oc.shape, F32),
+            jax.ShapeDtypeStruct((K, LA, ACB * BLK), F32),
+            jax.ShapeDtypeStruct((K, OL, OY, BLK), F32),
         ],
-        in_specs=[
-            pl.BlockSpec((K, LA, 2 * BLK), lambda q: (0, 0, q)),
-            pl.BlockSpec((2, LA, LA), lambda q: (q, 0, 0)),
-            pl.BlockSpec((K, 2 * BLK), lambda q: (0, q)),
-            pl.BlockSpec((4, OL, OY, BLK), lambda q: (q, 0, 0, 0)),
-            pl.BlockSpec((4, OY, BLK), lambda q: (q, 0, 0)),
-        ] + [vmem] * 8,
+        in_specs=[vmem] * len(arrays),
         out_specs=[
-            pl.BlockSpec((K, LA, 2 * BLK), lambda q: (0, 0, q)),
+            pl.BlockSpec((4, LA, ACB * BLK), lambda q: (q, 0, 0)),
             pl.BlockSpec((4, OL, OY, BLK), lambda q: (q, 0, 0, 0)),
         ],
         scratch_shapes=[
@@ -455,13 +489,13 @@
             pltpu.VMEM((4, OL, EXT_ROWS, EXT_COLS), F32),
             pltpu.VMEM((2, 3 * BLK, BLK), F32),
         ],
+        compiler_params=pltpu.CompilerParams(vmem_limit_bytes=20 * 2**20),
         name="step",
-    )(atm, mix, bottom, oc, top, vel, mask, *halos)
+    )(*arrays)
 
 
 def body(atm, mix, oc, vel, mask, inter, weights):
-    bottom, top, *halos = exchange(inter, atm, oc, vel, mask, weights)
-    return tuple(local_step(atm, mix, bottom, oc, top, vel, mask, halos))
+    return tuple(local_step(exchange(inter, atm, mix, oc, vel, mask, weights)))
 
 
 def solution(mesh):

time: 43.2 us -> 37.9 us (0.88)
  Pallas kernels: 42.4 us -> 37.2 us
    pallas_call x1, Pallas kernels: 13.1 us -> 9.82 us  [local_step(): pl.pallas_call(step_kernel, grid=(NQ,), out_shape=[jax.ShapeDtypeStruct((...]
    pallas_call x1, Pallas kernels: 29.3 us -> 27.4 us  [exchange(): pl.pallas_call(exchange_kernel, out_shape=[jax.ShapeDtypeStruct(s, F32) f...]
where the time goes in v2:
time: 37.9 us; the launch traced here: 37.8 us
  Pallas kernels  37.2 us (98%)
  between operations  0.64 us (2%)
    pallas_call x1, Pallas kernels, exchange(): pl.pallas_call(exchange_kernel, out_shape=[jax.ShapeDtypeStruct(s, F32) f...  27.4 us
    pallas_call x1, Pallas kernels, local_step(): pl.pallas_call(step_kernel, grid=(NQ,), out_shape=[jax.ShapeDtypeStruct((...  9.82 us

profile of v2, /device:TPU:1, one launch (start us, length us, event | category | flops | bytes accessed | tf_op | source)
XLA Modules:
  0.0 37.8 jit_solution(13813979165822241227)
XLA Ops:
  0.6 27.4 %exchange.1 = (f32[16,72,1024]{2,1,0:T(8,128)S(1)}, f32[8,72,128]{2,1,0:T(8,128)S(1)}, f32[128,128]{1,0:T(8,128)S(1)}, f32[16,4,32,128]{3,2,1,0:T(8,128)S(1)}, f...) custom-call(s32[3,72]{1,0:T(4,128)} %inter_hbm.1, ...), custom_call_target="tpu_custom_call" | custom-call | tf_op jit(solution)/shard_map/exchange/pallas_call | solution.py:339
  28.0 9.8 %step.1 = (f32[16,72,1024]{2,1,0:T(8,128)}, f32[16,4,32,128]{3,2,1,0:T(8,128)}) custom-call(f32[16,72,1024]{2,1,0:T(8,128)S(1)} %get-tuple-element.13.mixed, f32[8,72,128]{2,1,0:T(8,128)S(1)} %get-tuple-element.14.first_column, f32[128,128]{1,0:T(8,128)S(1)} %get-tuple-element.15.bottom, f32[16,4,32,128]{3,2,1,0:T(8,128)S(1)} %get-tuple-element.16.oc, ...), custom_call_target="tpu_custom_call" | custom-call | tf_op jit(solution)/shard_map/step/pallas_call | solution.py:475

commit v3 on v2

--- a/solution.py
+++ b/solution.py
@@ -18,8 +18,11 @@
 NSUB = 4
 SLOTS = 9 * CAP
 HW = NSUB
-EXT_ROWS = OY + 2 * HW
-EXT_COLS = 2 * BLK
+LANES = OY + 2 * HW
+TRIPLES = 6
+EARLY_GROUPS = TRIPLES * (OL - 1)
+COLS = BLK + 2 * HW
+PADDED = COLS + 16
 
 ocean_uptake = 0.5
 air_uptake = 0.5
@@ -33,7 +36,8 @@
 REQUEST, CONTRIB, SURFACE, EARLY, LATE = range(5)
 NQ = 4
 EARLY_ROWS = NQ * 48 + 16
-EARLY_STRIP = NQ * 16
+EARLY_STRIP = 80
+LATE_STRIP = 24
 
 
 def split2(x):
@@ -54,6 +58,37 @@
 
 def dot_nt(a, b):
     return lax.dot_general(a, b, (((1,), (1,)), ((), ())), preferred_element_type=F32)
+
+
+def turned(tiles):
+    gap = jnp.zeros((2 * HW, BLK), F32)
+    rows = []
+    for tile in tiles:
+        rows += [tile, gap]
+    full = jnp.concatenate(rows, 0)
+    if full.shape[0] < BLK:
+        full = jnp.concatenate([full, jnp.zeros((BLK - full.shape[0], BLK), F32)], 0)
+    return full.T
+
+
+def cut_edges(groups, strips, ends, lane):
+    blocks = {}
+    for n, full in groups:
+        strips[0, n * HW:(n + 1) * HW, :] = full[0:HW]
+        strips[1, n * HW:(n + 1) * HW, :] = full[BLK - HW:BLK]
+        edge = jnp.concatenate([full[0:HW], full[BLK - HW:BLK]], 0)
+        here = (lane % LANES) // HW == n % 10
+        low = pltpu.roll(edge, (n % 10) * HW, 1)
+        high = pltpu.roll(edge, ((n % 10) * HW - (OY - HW)) % BLK, 1)
+        old = blocks.get(n // 10, (jnp.zeros((8, BLK), F32),) * 2)
+        blocks[n // 10] = (jnp.where(here, low, old[0]), jnp.where(here, high, old[1]))
+    for b in range(2):
+        low, high = blocks.get(b, (jnp.zeros((8, BLK), F32),) * 2)
+        rows = slice(b * HW, (b + 1) * HW)
+        ends[0, rows, :] = low[0:HW]
+        ends[1, rows, :] = low[HW:8]
+        ends[2, rows, :] = high[0:HW]
+        ends[3, rows, :] = high[HW:8]
 
 
 def exchange_kernel(
@@ -111,8 +146,9 @@
     fields[2] = wet
     vel = fields
 
-    er[:, NQ * 48:2 * BLK, :] = jnp.zeros((2, 2 * BLK - NQ * 48, BLK), F32)
-    es[...] = jnp.zeros_like(es)
+    er[:, NQ * 48 + 8:EARLY_ROWS, :] = jnp.zeros((2, 8, BLK), F32)
+    es[:, 72:EARLY_STRIP, :] = jnp.zeros((2, 8, BLK), F32)
+    lane = lax.broadcasted_iota(jnp.int32, (8, BLK), 1)
     for q in range(NQ):
         for lev in range(1, OL):
             for p in range(4):
@@ -124,20 +160,11 @@
         field = vel[n] if n < 2 else wet
         er[0, row:row + HW, :] = field[0:HW]
         er[1, row:row + HW, :] = field[OY - HW:OY]
-    for q in range(NQ):
-        for lev in range(1, OL):
-            turned = oc[4 * q:4 * q + 4, lev].reshape(BLK, BLK).T
-            row = q * 16 + (lev - 1) * 4
-            es[0, row:row + HW, :] = turned[0:HW]
-            es[1, row:row + HW, :] = turned[BLK - HW:BLK]
-    turned = jnp.concatenate([vel[0], vel[1], wet, jnp.zeros_like(wet)], 0).T
-    es[0, 12:16, :] = turned[0:HW]
-    es[1, 12:16, :] = turned[BLK - HW:BLK]
-    for side in range(2):
-        for blk in range(2):
-            turned = er[side, blk * BLK:(blk + 1) * BLK, :].T
-            ec[2 * side, blk * HW:(blk + 1) * HW, :] = turned[0:HW]
-            ec[2 * side + 1, blk * HW:(blk + 1) * HW, :] = turned[BLK - HW:BLK]
+    groups = [
+        (t * 3 + lev - 1, turned([oc[k, lev] for k in range(3 * t, min(3 * t + 3, K))]))
+        for t in range(TRIPLES) for lev in range(1, OL)
+    ]
+    cut_edges(groups + [(EARLY_GROUPS, turned([vel[0], vel[1], wet]))], es, ec, lane)
 
     pl.semaphore_wait(barrier, len(NEIGHBOURS))
 
@@ -249,9 +276,6 @@
     place = chosen.T[0:OY].astype(BF16)
     for g in NEIGHBOURS:
         message(CONTRIB, g, cbuf.at[g], cin.at[g]).wait_recv()
-    lr[...] = jnp.zeros_like(lr)
-    ls[...] = jnp.zeros_like(ls)
-    lc[...] = jnp.zeros_like(lc)
     for k in range(0, K, 2):
         pair = jnp.concatenate(
             [cin[:, n * CAP:(n + 1) * CAP, :].reshape(SLOTS, BLK) for n in (k, k + 1)], 1
@@ -264,14 +288,10 @@
             oc[k + n, 0] = new
             lr[0, (k + n) * 4:(k + n) * 4 + 4, :] = new[0:HW]
             lr[1, (k + n) * 4:(k + n) * 4 + 4, :] = new[OY - HW:OY]
-    for q in range(NQ):
-        turned = oc[4 * q:4 * q + 4, 0].reshape(BLK, BLK).T
-        ls[0, q * 8:q * 8 + HW, :] = turned[0:HW]
-        ls[1, q * 8:q * 8 + HW, :] = turned[BLK - HW:BLK]
-    for side in range(2):
-        turned = lr[side].T
-        lc[2 * side, 0:HW, :] = turned[0:HW]
-        lc[2 * side + 1, 0:HW, :] = turned[BLK - HW:BLK]
+    groups = [
+        (t, turned([oc[k, 0] for k in range(3 * t, min(3 * t + 3, K))])) for t in range(TRIPLES)
+    ]
+    cut_edges(groups, ls, lc, lane)
     late = halo(LATE, lr, lc, ls, lr_in, lc_in, ls_in, 4 * K)
     for copy in late:
         copy.start()
@@ -334,7 +354,7 @@
     shapes = [
         (K, LA, ACB * BLK), (ACB, LA, BLK), (K * ACB, BLK), (K, OL, OY, BLK), (3, OY, BLK),
         (2, EARLY_ROWS, BLK), (4, 8, BLK), (2, EARLY_STRIP, BLK),
-        (2, 4 * K, BLK), (4, 8, BLK), (2, 8 * NQ, BLK),
+        (2, 4 * K, BLK), (4, 8, BLK), (2, LATE_STRIP, BLK),
     ]
     return pl.pallas_call(
         exchange_kernel,
@@ -357,12 +377,12 @@
             pltpu.VMEM((9, (K + 1) * CAP, BLK), F32),
             pltpu.VMEM((9, (K + 1) * CAP, BLK), F32),
             pltpu.VMEM((ACB, K + 8, BLK), F32),
-            pltpu.VMEM((2, 2 * BLK, BLK), F32),
+            pltpu.VMEM((2, EARLY_ROWS, BLK), F32),
             pltpu.VMEM((4, 8, BLK), F32),
             pltpu.VMEM((2, EARLY_STRIP, BLK), F32),
-            pltpu.VMEM((2, BLK, BLK), F32),
+            pltpu.VMEM((2, 4 * K, BLK), F32),
             pltpu.VMEM((4, 8, BLK), F32),
-            pltpu.VMEM((2, 8 * NQ, BLK), F32),
+            pltpu.VMEM((2, LATE_STRIP, BLK), F32),
             pltpu.SemaphoreType.DMA((8,)),
             pltpu.SemaphoreType.DMA((8,)),
             pltpu.SemaphoreType.DMA((6,)),
@@ -381,113 +401,150 @@
 
 def step_kernel(
     mixed, first_column, bottom, oc, own, er, ec, es, lr, lc, ls,
-    atm_out, oc_out, coef, xs, ct,
+    atm_out, oc_out, atm_stage, oc_stage, coef, state, work, asem, osem,
 ):
-    q = pl.program_id(0)
-
-    def spread(east, west):
-        gap = jnp.zeros((BLK - 2 * HW, BLK), F32)
-        return jnp.concatenate([east, gap, west], 0).T
-
-    @pl.when(q == 0)
-    def _():
-        for side in range(2):
-            for blk in range(2):
-                ct[side, blk * BLK:(blk + 1) * BLK, :] = spread(
-                    ec[2 * side, blk * HW:(blk + 1) * HW, :],
-                    ec[2 * side + 1, blk * HW:(blk + 1) * HW, :],
-                )
-            ct[side, 2 * BLK:3 * BLK, :] = spread(lc[2 * side, 0:HW, :], lc[2 * side + 1, 0:HW, :])
-        ends = spread(es[0, 12:16, :], es[1, 12:16, :])
-        fields = []
-        for n in range(3):
-            row = NQ * 48 + n * 4
-            left = jnp.concatenate([own[n], er[0, row:row + HW, :], er[1, row:row + HW, :]], 0)
-            right = jnp.concatenate(
-                [ends[n * OY:(n + 1) * OY], ct[0, row:row + HW, :], ct[1, row:row + HW, :]], 0
-            )
-            fields.append(jnp.concatenate([left, right], 1))
-        u, v, wet = fields
-        coef[0] = wet * (mix_horizontal - 0.5 * u)
-        coef[1] = wet * (mix_horizontal + 0.5 * u)
-        coef[2] = wet * (mix_horizontal - 0.5 * v)
-        coef[3] = wet * (mix_horizontal + 0.5 * v)
-        coef[4] = wet * mix_vertical
-        coef[5] = wet * (1.0 - 4.0 * mix_horizontal - 2.0 * mix_vertical)
-        coef[6] = wet
-
-    for lev in range(OL):
-        if lev == 0:
-            base = pl.multiple_of(q * 16, 16)
-            north, south = lr[0, pl.ds(base, 16), :], lr[1, pl.ds(base, 16), :]
-            corner = pl.multiple_of(2 * BLK + q * 16, 16)
-            group = pl.multiple_of(q * 8, 8)
-            ends = spread(ls[0, pl.ds(group, 8), :][0:HW], ls[1, pl.ds(group, 8), :][0:HW])
-        else:
-            base = pl.multiple_of(q * 48 + (lev - 1) * 16, 16)
-            north, south = er[0, pl.ds(base, 16), :], er[1, pl.ds(base, 16), :]
-            corner = base
-            group = pl.multiple_of(q * 16, 16)
-            piece = slice((lev - 1) * HW, lev * HW)
-            ends = spread(es[0, pl.ds(group, 16), :][piece], es[1, pl.ds(group, 16), :][piece])
-        north_ends, south_ends = ct[0, pl.ds(corner, 16), :], ct[1, pl.ds(corner, 16), :]
-        for p in range(4):
-            part = slice(p * 4, p * 4 + 4)
-            xs[p, lev, 0:OY, 0:BLK] = oc[4 * q + p, lev]
-            xs[p, lev, OY:OY + HW, 0:BLK] = north[part]
-            xs[p, lev, OY + HW:EXT_ROWS, 0:BLK] = south[part]
-            xs[p, lev, 0:OY, BLK:EXT_COLS] = ends[p * OY:(p + 1) * OY]
-            xs[p, lev, OY:OY + HW, BLK:EXT_COLS] = north_ends[part]
-            xs[p, lev, OY + HW:EXT_ROWS, BLK:EXT_COLS] = south_ends[part]
-
-    def ocean(p, carry):
-        levels = [xs[p, lev] * coef[6] for lev in range(OL)]
-        for _ in range(NSUB):
-            new = []
-            for lev in range(OL):
-                x = levels[lev]
-                above, below = levels[max(lev - 1, 0)], levels[min(lev + 1, OL - 1)]
-                new.append(
-                    coef[0] * pltpu.roll(x, EXT_COLS - 1, 1)
-                    + coef[1] * pltpu.roll(x, 1, 1)
-                    + coef[2] * pltpu.roll(x, EXT_ROWS - 1, 0)
-                    + coef[3] * pltpu.roll(x, 1, 0)
-                    + coef[4] * (above + below)
-                    + coef[5] * x
-                )
-            levels = new
-        for lev in range(OL):
-            oc_out[p, lev] = levels[lev][0:OY, 0:BLK]
-        return carry
-
-    lax.fori_loop(0, 4, ocean, 0)
-
-    for p in range(4):
-        k = 4 * q + p
+    def surface_part(k, carry):
         surface = bottom[pl.ds(pl.multiple_of(k * ACB, ACB), ACB), :]
         for b in range(ACB):
             cols = slice(b * BLK, (b + 1) * BLK)
-            atm_out[p, :, cols] = mixed[k, :, cols] + first_column[b] * surface[b:b + 1]
+            atm_stage[k, :, cols] = mixed[k, :, cols] + first_column[b] * surface[b:b + 1]
+        pltpu.make_async_copy(atm_stage.at[k], atm_out.at[k], asem.at[k]).start()
+        return carry
+
+    lax.fori_loop(0, K, surface_part, 0)
+
+    lane = lax.broadcasted_iota(jnp.int32, (8, BLK), 1)
+    shifted = (lane + HW) % BLK
+    north = (shifted % LANES >= OY + HW) & (shifted < 3 * LANES)
+    south = (shifted % LANES < HW) & (shifted < 3 * LANES)
+
+    def widen(tiles, norths, souths):
+        gap = jnp.zeros((HW, BLK), F32)
+        rows = []
+        for n in range(3):
+            n_row = norths[n] if n < len(tiles) else gap
+            s_row = souths[n + 1] if n + 1 < len(tiles) else gap
+            rows += [tiles[n] if n < len(tiles) else jnp.zeros((OY, BLK), F32), n_row, s_row]
+        return jnp.concatenate(rows + [gap, souths[0]], 0).T
+
+    def edges(strips, ends, n):
+        rows = slice((n // 10) * HW, (n // 10 + 1) * HW)
+        mine = jnp.concatenate(
+            [strips[0, n * HW:(n + 1) * HW, :], strips[1, n * HW:(n + 1) * HW, :]], 0
+        )
+        above = jnp.concatenate([ends[0, rows, :], ends[1, rows, :]], 0)
+        below = jnp.concatenate([ends[2, rows, :], ends[3, rows, :]], 0)
+        above = pltpu.roll(above, (OY - (n % 10) * HW) % BLK, 1)
+        below = pltpu.roll(below, (BLK - HW - (n % 10) * HW) % BLK, 1)
+        return jnp.where(north, above, jnp.where(south, below, mine))
+
+    fields = []
+    ends = edges(es, ec, EARLY_GROUPS)
+    for n in range(3):
+        row = NQ * 48 + n * HW
+        inner = widen([own[n]] * 3, [er[0, row:row + HW, :]] * 3, [er[1, row:row + HW, :]] * 3)
+        parts = [pltpu.roll(ends, ((m - n) * LANES) % BLK, 1) for m in range(3)]
+        outer = jnp.where(
+            shifted < LANES, parts[0], jnp.where(shifted < 2 * LANES, parts[1], parts[2])
+        )
+        fields.append(jnp.concatenate([inner, outer], 0))
+    u, v, wet = fields
+    coef[0] = wet * (mix_horizontal - 0.5 * u)
+    coef[1] = wet * (mix_horizontal + 0.5 * u)
+    coef[2] = wet * (mix_horizontal - 0.5 * v)
+    coef[3] = wet * (mix_horizontal + 0.5 * v)
+    coef[4] = wet * mix_vertical
+    coef[5] = wet * (1.0 - 4.0 * mix_horizontal - 2.0 * mix_vertical)
+    coef[6] = wet
+
+    for t in range(TRIPLES):
+        ks = range(3 * t, min(3 * t + 3, K))
+        for lev in range(OL):
+            if lev == 0:
+                halo = [[lr[side, k * HW:(k + 1) * HW, :] for k in ks] for side in range(2)]
+                outer = edges(ls, lc, t)
+            else:
+                rows = [(k // 4) * 48 + (lev - 1) * 16 + (k % 4) * HW for k in ks]
+                halo = [[er[side, row:row + HW, :] for row in rows] for side in range(2)]
+                outer = edges(es, ec, t * 3 + lev - 1)
+            inner = widen([oc[k, lev] for k in ks], *halo) * coef[6, 0:BLK, :]
+            outer = outer * coef[6, BLK:COLS, :]
+            state[t, lev, 0:8, :] = outer
+            state[t, lev, 8:8 + BLK, :] = inner
+            state[t, lev, 8 + BLK:8 + COLS, :] = outer
+            state[t, lev, 8 + COLS:PADDED, :] = inner[0:8]
+
+    def ocean(t, carry):
+        for sub in range(NSUB):
+            def source(lev, start):
+                if sub == 0:
+                    return state[t, lev, start:start + 8, :]
+                return work[(sub - 1) % 2, lev, start:start + 8, :]
+
+            for tile in range(COLS // 8):
+                start = 8 + tile * 8
+                c = [coef[n, tile * 8:tile * 8 + 8, :] for n in range(6)]
+                x = [source(lev, start) for lev in range(OL)]
+                for lev in range(OL):
+                    new = (
+                        c[0] * source(lev, start + 1)
+                        + c[1] * source(lev, start - 1)
+                        + c[2] * pltpu.roll(x[lev], BLK - 1, 1)
+                        + c[3] * pltpu.roll(x[lev], 1, 1)
+                        + c[4] * (x[max(lev - 1, 0)] + x[min(lev + 1, OL - 1)])
+                        + c[5] * x[lev]
+                    )
+                    work[sub % 2, lev, start:start + 8, :] = new
+                    if tile == 0:
+                        work[sub % 2, lev, 8 + COLS:PADDED, :] = new
+                    if tile == COLS // 8 - 1:
+                        work[sub % 2, lev, 0:8, :] = new
+        for lev in range(OL):
+            out = work[(NSUB - 1) % 2, lev, 8:8 + BLK, :].T
+            for n in range(3):
+                oc_stage[3 * t + n, lev] = out[n * LANES:n * LANES + OY]
+
+        @pl.when(t < TRIPLES - 1)
+        def _():
+            pltpu.make_async_copy(
+                oc_stage.at[pl.ds(3 * t, 3)], oc_out.at[pl.ds(3 * t, 3)], osem.at[t]
+            ).start()
+
+        return carry
+
+    lax.fori_loop(0, TRIPLES, ocean, 0)
+    last = pltpu.make_async_copy(
+        oc_stage.at[pl.ds(K - 1, 1)], oc_out.at[pl.ds(K - 1, 1)], osem.at[TRIPLES - 1]
+    )
+    last.start()
+    for k in range(K):
+        pltpu.make_async_copy(atm_stage.at[k], atm_out.at[k], asem.at[k]).wait()
+    for t in range(TRIPLES - 1):
+        pltpu.make_async_copy(
+            oc_stage.at[pl.ds(3 * t, 3)], oc_out.at[pl.ds(3 * t, 3)], osem.at[t]
+        ).wait()
+    last.wait()
 
 
 def local_step(arrays):
     vmem = pl.BlockSpec(memory_space=pltpu.VMEM)
+    hbm = pl.BlockSpec(memory_space=pltpu.HBM)
     return pl.pallas_call(
         step_kernel,
-        grid=(NQ,),
         out_shape=[
             jax.ShapeDtypeStruct((K, LA, ACB * BLK), F32),
             jax.ShapeDtypeStruct((K, OL, OY, BLK), F32),
         ],
         in_specs=[vmem] * len(arrays),
-        out_specs=[
-            pl.BlockSpec((4, LA, ACB * BLK), lambda q: (q, 0, 0)),
-            pl.BlockSpec((4, OL, OY, BLK), lambda q: (q, 0, 0, 0)),
-        ],
+        out_specs=[hbm, hbm],
         scratch_shapes=[
-            pltpu.VMEM((7, EXT_ROWS, EXT_COLS), F32),
-            pltpu.VMEM((4, OL, EXT_ROWS, EXT_COLS), F32),
-            pltpu.VMEM((2, 3 * BLK, BLK), F32),
+            pltpu.VMEM((K, LA, ACB * BLK), F32),
+            pltpu.VMEM((3 * TRIPLES, OL, OY, BLK), F32),
+            pltpu.VMEM((7, COLS, BLK), F32),
+            pltpu.VMEM((TRIPLES, OL, PADDED, BLK), F32),
+            pltpu.VMEM((2, OL, PADDED, BLK), F32),
+            pltpu.SemaphoreType.DMA((K,)),
+            pltpu.SemaphoreType.DMA((TRIPLES,)),
         ],
         compiler_params=pltpu.CompilerParams(vmem_limit_bytes=20 * 2**20),
         name="step",

time: 37.9 us -> 34.8 us (0.918)
  Pallas kernels: 37.2 us -> 34.1 us
    pallas_call x1, Pallas kernels: 9.82 us -> 6.67 us  [local_step(): pl.pallas_call(step_kernel, out_shape=[jax.ShapeDtypeStruct((K, LA, ACB *...]
where the time goes in v3:
time: 34.8 us; the launch traced here: 34.7 us
  Pallas kernels  34.1 us (98%)
  between operations  0.64 us (2%)
    pallas_call x1, Pallas kernels, exchange(): pl.pallas_call(exchange_kernel, out_shape=[jax.ShapeDtypeStruct(s, F32) f...  27.4 us
    pallas_call x1, Pallas kernels, local_step(): pl.pallas_call(step_kernel, out_shape=[jax.ShapeDtypeStruct((K, LA, ACB *...  6.67 us

profile of v3, /device:TPU:1, one launch (start us, length us, event | category | flops | bytes accessed | tf_op | source)
XLA Modules:
  0.0 34.7 jit_solution(5638850630025731489)
XLA Ops:
  0.6 27.4 %exchange.1 = (f32[16,72,1024]{2,1,0:T(8,128)S(1)}, f32[8,72,128]{2,1,0:T(8,128)S(1)}, f32[128,128]{1,0:T(8,128)S(1)}, f32[16,4,32,128]{3,2,1,0:T(8,128)S(1)}, f...) custom-call(s32[3,72]{1,0:T(4,128)} %inter_hbm.1, ...), custom_call_target="tpu_custom_call" | custom-call | tf_op jit(solution)/shard_map/exchange/pallas_call | solution.py:359
  28.0 6.7 %step.1 = (f32[16,72,1024]{2,1,0:T(8,128)}, f32[16,4,32,128]{3,2,1,0:T(8,128)}) custom-call(f32[16,72,1024]{2,1,0:T(8,128)S(1)} %get-tuple-element.13.mixed, f32[8,72,128]{2,1,0:T(8,128)S(1)} %get-tuple-element.14.first_column, f32[128,128]{1,0:T(8,128)S(1)} %get-tuple-element.15.bottom, f32[16,4,32,128]{3,2,1,0:T(8,128)S(1)} %get-tuple-element.16.oc, ...), custom_call_target="tpu_custom_call" | custom-call | tf_op jit(solution)/shard_map/step/pallas_call | solution.py:532

commit v4 on v3

--- a/solution.py
+++ b/solution.py
@@ -36,7 +36,7 @@
 REQUEST, CONTRIB, SURFACE, EARLY, LATE = range(5)
 NQ = 4
 EARLY_ROWS = NQ * 48 + 16
-EARLY_STRIP = 80
+EARLY_STRIP = 96
 LATE_STRIP = 24
 
 
@@ -91,12 +91,68 @@
         ends[3, rows, :] = high[HW:8]
 
 
+def widen(tiles, norths, souths):
+    gap = jnp.zeros((HW, BLK), F32)
+    rows = []
+    for n in range(3):
+        n_row = norths[n] if n < len(tiles) else gap
+        s_row = souths[n + 1] if n + 1 < len(tiles) else gap
+        rows += [tiles[n] if n < len(tiles) else jnp.zeros((OY, BLK), F32), n_row, s_row]
+    return jnp.concatenate(rows + [gap, souths[0]], 0).T
+
+
+def outer_columns(strips, ends, n, lane):
+    shifted = (lane + HW) % BLK
+    north = (shifted % LANES >= OY + HW) & (shifted < 3 * LANES)
+    south = (shifted % LANES < HW) & (shifted < 3 * LANES)
+    rows = slice((n // 10) * HW, (n // 10 + 1) * HW)
+    mine = jnp.concatenate(
+        [strips[0, n * HW:(n + 1) * HW, :], strips[1, n * HW:(n + 1) * HW, :]], 0
+    )
+    above = jnp.concatenate([ends[0, rows, :], ends[1, rows, :]], 0)
+    below = jnp.concatenate([ends[2, rows, :], ends[3, rows, :]], 0)
+    above = pltpu.roll(above, (OY - (n % 10) * HW) % BLK, 1)
+    below = pltpu.roll(below, (BLK - HW - (n % 10) * HW) % BLK, 1)
+    return jnp.where(north, above, jnp.where(south, below, mine))
+
+
+def store_tile(state, coef, t, lev, inner, outer):
+    inner = inner * coef[6, 0:BLK, :]
+    outer = outer * coef[6, BLK:COLS, :]
+    state[t, lev, 0:8, :] = outer
+    state[t, lev, 8:8 + BLK, :] = inner
+    state[t, lev, 8 + BLK:8 + COLS, :] = outer
+    state[t, lev, 8 + COLS:PADDED, :] = inner[0:8]
+
+
+def set_coefficients(coef, own, er, ends, lane):
+    shifted = (lane + HW) % BLK
+    fields = []
+    for n in range(3):
+        row = NQ * 48 + n * HW
+        inner = widen([own[n]] * 3, [er[0, row:row + HW, :]] * 3, [er[1, row:row + HW, :]] * 3)
+        parts = [pltpu.roll(ends, ((m - n) * LANES) % BLK, 1) for m in range(3)]
+        outer = jnp.where(
+            shifted < LANES, parts[0], jnp.where(shifted < 2 * LANES, parts[1], parts[2])
+        )
+        fields.append(jnp.concatenate([inner, outer], 0))
+    u, v, wet = fields
+    coef[0] = wet * (mix_horizontal - 0.5 * u)
+    coef[1] = wet * (mix_horizontal + 0.5 * u)
+    coef[2] = wet * (mix_horizontal - 0.5 * v)
+    coef[3] = wet * (mix_horizontal + 0.5 * v)
+    coef[4] = wet * mix_vertical
+    coef[5] = wet * (1.0 - 4.0 * mix_horizontal - 2.0 * mix_vertical)
+    coef[6] = wet
+
+
 def exchange_kernel(
     inter_hbm, atm_hbm, mix_hbm, oc_hbm, vel_hbm, mask_hbm, w_hbm,
-    mixed, first_column, bottom, oc, fields, er_in, ec_in, es_in, lr_in, lc_in, ls_in,
-    inter, wbuf, abuf, xbuf, mbuf, maskbuf, stacked, ast, req, reqs, cbuf, cin, sbuf, sin, acc,
-    er, ec, es, lr, lc, ls,
-    wsem, xsem, lsem, ssem, rsem,
+    mixed, first_column, bottom, coef, state,
+    inter, oc, fields, wbuf, abuf, xbuf, mbuf, maskbuf, stacked, ast,
+    req, reqs, cbuf, cin, sbuf, sin, acc,
+    er, ec, es, lr, lc, ls, er_in, ec_in, es_in, lr_in, lc_in, ls_in,
+    wsem, xsem, lsem, ssem, rsem, surf_sem,
 ):
     nx, ny = lax.axis_size("gx"), lax.axis_size("gy")
     i, j = lax.axis_index("gx"), lax.axis_index("gy")
@@ -107,15 +163,23 @@
 
     def message(kind, g, src, dst, sign=1):
         return pltpu.make_async_remote_copy(
-            src_ref=src, dst_ref=dst, send_sem=ssem.at[kind, g], recv_sem=rsem.at[kind, g],
+            src_ref=src, dst_ref=dst, send_sem=ssem.at[kind],
+            recv_sem=surf_sem.at[g] if kind == SURFACE else rsem.at[kind],
             device_id=device(g, sign), device_id_type=MESH,
         )
+
+    def all_of(kind, sem, span):
+        pltpu.make_async_copy(span, span, sem.at[kind]).wait()
+
+    spans = {
+        REQUEST: req.at[pl.ds(0, 8)], CONTRIB: cbuf.at[pl.ds(0, 8)], SURFACE: sbuf.at[pl.ds(0, 8)],
+        EARLY: wbuf.at[pl.ds(0, 5)], LATE: er.at[0],
+    }
 
     barrier = pltpu.get_barrier_semaphore()
     for g in NEIGHBOURS:
         pl.semaphore_signal(barrier, inc=1, device_id=device(g, 1), device_id_type=MESH)
 
-    chunk = WSL // 8
     small = [
         pltpu.make_async_copy(src, dst, lsem.at[n])
         for n, (src, dst) in enumerate((
@@ -123,23 +187,59 @@
             (atm_hbm.at[:, pl.ds(0, 8), :], abuf), (mix_hbm, mbuf), (inter_hbm, inter),
         ))
     ]
-    loads = [
-        pltpu.make_async_copy(
-            w_hbm.at[pl.ds(c * chunk, chunk)], wbuf.at[pl.ds(c * chunk, chunk)], wsem.at[c]
-        )
-        for c in range(8)
-    ]
-    columns = [
-        pltpu.make_async_copy(atm_hbm.at[pl.ds(2 * c, 2)], xbuf.at[pl.ds(2 * c, 2)], xsem.at[c])
-        for c in range(8)
-    ]
-    for load in small[5:6] + small[0:5] + loads:
-        load.start()
+    weights = pltpu.make_async_copy(w_hbm, wbuf, wsem)
+    columns = pltpu.make_async_copy(atm_hbm, xbuf, xsem)
+    small[5].start()
+    small[3].start()
+    weights.start()
 
     small[5].wait()
     for e in range(SLOTS):
         req[e // CAP, pl.ds(e % CAP, 1), :] = jnp.full((1, BLK), inter[1, e], jnp.int32)
     reqs[4] = req[4]
+
+    small[3].wait()
+    for b in range(ACB):
+        block = abuf[:, 0, b * BLK:(b + 1) * BLK]
+        hi, lo = split2(block)
+        ast[b, 0:K, :] = hi
+        ast[b, K:2 * K, :] = lo
+    for load in small[0:3] + small[4:5]:
+        load.start()
+    weights.wait()
+    columns.start()
+
+    def contrib_rows(g):
+        for s in range(CAP):
+            e = g * CAP + s
+            hi, lo = split2(wbuf[jnp.maximum(inter[2, e], 0)])
+            a = ast[jnp.maximum(inter[0, e], 0)]
+            first = dot_nt(a, hi)
+            second = dot_nt(a[0:K], lo)
+            cbuf[g, pl.ds(s, K, stride=CAP), :] = first[0:K] + first[K:2 * K] + second
+
+    contrib_rows(NEIGHBOURS[0])
+    pl.semaphore_wait(barrier, len(NEIGHBOURS))
+
+    requests = [message(REQUEST, g, req.at[g], reqs.at[g]) for g in NEIGHBOURS]
+    for copy in requests:
+        copy.start()
+
+    message(CONTRIB, NEIGHBOURS[0], cbuf.at[NEIGHBOURS[0]], cin.at[NEIGHBOURS[0]]).start()
+
+    def contrib_group(t, carry):
+        g = (t // 2) * (1 - t % 2) + (8 - t // 2) * (t % 2)
+        contrib_rows(g)
+
+        @pl.when(g != 4)
+        def _():
+            message(CONTRIB, g, cbuf.at[g], cin.at[g]).start()
+
+        return carry
+
+    lax.fori_loop(1, 9, contrib_group, 0)
+    cin[4] = cbuf[4]
+
     for load in small[0:3]:
         load.wait()
     wet = maskbuf[...].astype(F32)
@@ -147,7 +247,7 @@
     vel = fields
 
     er[:, NQ * 48 + 8:EARLY_ROWS, :] = jnp.zeros((2, 8, BLK), F32)
-    es[:, 72:EARLY_STRIP, :] = jnp.zeros((2, 8, BLK), F32)
+    es[:, 72:EARLY_STRIP, :] = jnp.zeros((2, EARLY_STRIP - 72, BLK), F32)
     lane = lax.broadcasted_iota(jnp.int32, (8, BLK), 1)
     for q in range(NQ):
         for lev in range(1, OL):
@@ -166,12 +266,6 @@
     ]
     cut_edges(groups + [(EARLY_GROUPS, turned([vel[0], vel[1], wet]))], es, ec, lane)
 
-    pl.semaphore_wait(barrier, len(NEIGHBOURS))
-
-    requests = [message(REQUEST, g, req.at[g], reqs.at[g]) for g in NEIGHBOURS]
-    for copy in requests:
-        copy.start()
-
     sides = {1: 0, 7: 1}
     ends = {3: 0, 5: 1}
     corners = {0: 0, 2: 1, 6: 2, 8: 3}
@@ -194,38 +288,7 @@
     for copy in early:
         copy.start()
 
-    small[3].wait()
-    for b in range(ACB):
-        block = abuf[:, 0, b * BLK:(b + 1) * BLK]
-        hi, lo = split2(block)
-        ast[b, 0:K, :] = hi
-        ast[b, K:2 * K, :] = lo
-    for load in loads:
-        load.wait()
-    for load in columns:
-        load.start()
-
-    def contrib_group(t, carry):
-        g = (t // 2) * (1 - t % 2) + (8 - t // 2) * (t % 2)
-        for s in range(CAP):
-            e = g * CAP + s
-            hi, lo = split2(wbuf[jnp.maximum(inter[2, e], 0)])
-            a = ast[jnp.maximum(inter[0, e], 0)]
-            first = dot_nt(a, hi)
-            second = dot_nt(a[0:K], lo)
-            cbuf[g, pl.ds(s, K, stride=CAP), :] = first[0:K] + first[K:2 * K] + second
-
-        @pl.when(g != 4)
-        def _():
-            message(CONTRIB, g, cbuf.at[g], cin.at[g]).start()
-
-        return carry
-
-    lax.fori_loop(0, 9, contrib_group, 0)
-    cin[4] = cbuf[4]
-
-    for copy in requests:
-        copy.wait_recv()
+    all_of(REQUEST, rsem, spans[REQUEST])
     lanes = lax.broadcasted_iota(jnp.int32, (SLOTS, BLK), 1)
     chosen = (reqs[...].reshape(SLOTS, BLK) == lanes).astype(F32)
     pick = chosen[:, 0:OY].astype(BF16)
@@ -251,8 +314,7 @@
         stacked[b] = (mh + pltpu.roll(mh, 80, 1) + pltpu.roll(m - mh, 160, 1)).astype(BF16)
     upper = lax.broadcasted_iota(jnp.int32, (8, BLK), 0) > 0
 
-    for c in range(8):
-        columns[c].wait()
+    columns.wait()
 
     def mixing(c, carry):
         for b in range(ACB):
@@ -274,8 +336,7 @@
     lax.fori_loop(0, 8, mixing, 0)
 
     place = chosen.T[0:OY].astype(BF16)
-    for g in NEIGHBOURS:
-        message(CONTRIB, g, cbuf.at[g], cin.at[g]).wait_recv()
+    all_of(CONTRIB, rsem, spans[CONTRIB])
     for k in range(0, K, 2):
         pair = jnp.concatenate(
             [cin[:, n * CAP:(n + 1) * CAP, :].reshape(SLOTS, BLK) for n in (k, k + 1)], 1
@@ -296,11 +357,25 @@
     for copy in late:
         copy.start()
 
+
+    all_of(EARLY, rsem, spans[EARLY])
+    set_coefficients(coef, fields, er_in, outer_columns(es_in, ec_in, EARLY_GROUPS, lane), lane)
+    for t in range(TRIPLES):
+        ks = range(3 * t, min(3 * t + 3, K))
+        for lev in range(1, OL):
+            rows = [(k // 4) * 48 + (lev - 1) * 16 + (k % 4) * HW for k in ks]
+            norths, souths = ([er_in[side, row:row + HW, :] for row in rows] for side in range(2))
+            store_tile(
+                state, coef, t, lev, widen([oc[k, lev] for k in ks], norths, souths),
+                outer_columns(es_in, ec_in, t * 3 + lev - 1, lane),
+            )
+
     acc[...] = jnp.zeros_like(acc)
 
     def return_group(t, carry):
-        t = (t + 8) % 9
-        g = (t // 2) * (1 - t % 2) + (8 - t // 2) * (t % 2)
+        near = (8 - t) // 6
+        u = (t + 6) % 9
+        g = near * (3 + t) + (1 - near) * ((u // 2) * (1 - u % 2) + (8 - u // 2) * (u % 2))
 
         @pl.when(g != 4)
         def _():
@@ -337,22 +412,27 @@
             acc[b, 0:K, :] - acc[b, K:K + 1, :] * old
         )
 
-    for copy in requests:
-        copy.wait_send()
-    for copy in early:
-        copy.wait()
-    for copy in late:
-        copy.wait()
-    for g in NEIGHBOURS:
-        message(CONTRIB, g, cbuf.at[g], cin.at[g]).wait_send()
-        message(SURFACE, g, sbuf.at[g], sin.at[g], -1).wait_send()
+    all_of(LATE, rsem, spans[LATE])
+    for t in range(TRIPLES):
+        ks = range(3 * t, min(3 * t + 3, K))
+        norths, souths = ([lr_in[side, k * HW:(k + 1) * HW, :] for k in ks] for side in range(2))
+        store_tile(
+            state, coef, t, 0, widen([oc[k, 0] for k in ks], norths, souths),
+            outer_columns(ls_in, lc_in, t, lane),
+        )
+
+    for kind in range(5):
+        all_of(kind, ssem, spans[kind])
 
 
 def exchange(inter, atm, mix, oc, vel, mask, weights):
     vmem = pl.BlockSpec(memory_space=pltpu.VMEM)
     hbm = pl.BlockSpec(memory_space=pltpu.HBM)
     shapes = [
-        (K, LA, ACB * BLK), (ACB, LA, BLK), (K * ACB, BLK), (K, OL, OY, BLK), (3, OY, BLK),
+        (K, LA, ACB * BLK), (ACB, LA, BLK), (K * ACB, BLK),
+        (7, COLS, BLK), (TRIPLES, OL, PADDED, BLK),
+    ]
+    halos = [
         (2, EARLY_ROWS, BLK), (4, 8, BLK), (2, EARLY_STRIP, BLK),
         (2, 4 * K, BLK), (4, 8, BLK), (2, LATE_STRIP, BLK),
     ]
@@ -363,6 +443,8 @@
         out_specs=[vmem] * len(shapes),
         scratch_shapes=[
             pltpu.SMEM((3, SLOTS), jnp.int32),
+            pltpu.VMEM((K, OL, OY, BLK), F32),
+            pltpu.VMEM((3, OY, BLK), F32),
             pltpu.VMEM((WSL, BLK, BLK), F32),
             pltpu.VMEM((K, 8, ACB * BLK), F32),
             pltpu.VMEM((K, LA, ACB * BLK), F32),
@@ -377,17 +459,13 @@
             pltpu.VMEM((9, (K + 1) * CAP, BLK), F32),
             pltpu.VMEM((9, (K + 1) * CAP, BLK), F32),
             pltpu.VMEM((ACB, K + 8, BLK), F32),
-            pltpu.VMEM((2, EARLY_ROWS, BLK), F32),
-            pltpu.VMEM((4, 8, BLK), F32),
-            pltpu.VMEM((2, EARLY_STRIP, BLK), F32),
-            pltpu.VMEM((2, 4 * K, BLK), F32),
-            pltpu.VMEM((4, 8, BLK), F32),
-            pltpu.VMEM((2, LATE_STRIP, BLK), F32),
-            pltpu.SemaphoreType.DMA((8,)),
-            pltpu.SemaphoreType.DMA((8,)),
+            *[pltpu.VMEM(shape, F32) for shape in halos * 2],
+            pltpu.SemaphoreType.DMA,
+            pltpu.SemaphoreType.DMA,
             pltpu.SemaphoreType.DMA((6,)),
-            pltpu.SemaphoreType.DMA((5, 9)),
-            pltpu.SemaphoreType.DMA((5, 9)),
+            pltpu.SemaphoreType.DMA((5,)),
+            pltpu.SemaphoreType.DMA((5,)),
+            pltpu.SemaphoreType.DMA((9,)),
         ],
         compiler_params=pltpu.CompilerParams(
             collective_id=0, has_side_effects=True, vmem_limit_bytes=30 * 2**20
@@ -400,8 +478,8 @@
 
 
 def step_kernel(
-    mixed, first_column, bottom, oc, own, er, ec, es, lr, lc, ls,
-    atm_out, oc_out, atm_stage, oc_stage, coef, state, work, asem, osem,
+    mixed, first_column, bottom, coef, state,
+    atm_out, oc_out, atm_stage, oc_stage, work, asem, osem,
 ):
     def surface_part(k, carry):
         surface = bottom[pl.ds(pl.multiple_of(k * ACB, ACB), ACB), :]
@@ -412,67 +490,6 @@
         return carry
 
     lax.fori_loop(0, K, surface_part, 0)
-
-    lane = lax.broadcasted_iota(jnp.int32, (8, BLK), 1)
-    shifted = (lane + HW) % BLK
-    north = (shifted % LANES >= OY + HW) & (shifted < 3 * LANES)
-    south = (shifted % LANES < HW) & (shifted < 3 * LANES)
-
-    def widen(tiles, norths, souths):
-        gap = jnp.zeros((HW, BLK), F32)
-        rows = []
-        for n in range(3):
-            n_row = norths[n] if n < len(tiles) else gap
-            s_row = souths[n + 1] if n + 1 < len(tiles) else gap
-            rows += [tiles[n] if n < len(tiles) else jnp.zeros((OY, BLK), F32), n_row, s_row]
-        return jnp.concatenate(rows + [gap, souths[0]], 0).T
-
-    def edges(strips, ends, n):
-        rows = slice((n // 10) * HW, (n // 10 + 1) * HW)
-        mine = jnp.concatenate(
-            [strips[0, n * HW:(n + 1) * HW, :], strips[1, n * HW:(n + 1) * HW, :]], 0
-        )
-        above = jnp.concatenate([ends[0, rows, :], ends[1, rows, :]], 0)
-        below = jnp.concatenate([ends[2, rows, :], ends[3, rows, :]], 0)
-        above = pltpu.roll(above, (OY - (n % 10) * HW) % BLK, 1)
-        below = pltpu.roll(below, (BLK - HW - (n % 10) * HW) % BLK, 1)
-        return jnp.where(north, above, jnp.where(south, below, mine))
-
-    fields = []
-    ends = edges(es, ec, EARLY_GROUPS)
-    for n in range(3):
-        row = NQ * 48 + n * HW
-        inner = widen([own[n]] * 3, [er[0, row:row + HW, :]] * 3, [er[1, row:row + HW, :]] * 3)
-        parts = [pltpu.roll(ends, ((m - n) * LANES) % BLK, 1) for m in range(3)]
-        outer = jnp.where(
-            shifted < LANES, parts[0], jnp.where(shifted < 2 * LANES, parts[1], parts[2])
-        )
-        fields.append(jnp.concatenate([inner, outer], 0))
-    u, v, wet = fields
-    coef[0] = wet * (mix_horizontal - 0.5 * u)
-    coef[1] = wet * (mix_horizontal + 0.5 * u)
-    coef[2] = wet * (mix_horizontal - 0.5 * v)
-    coef[3] = wet * (mix_horizontal + 0.5 * v)
-    coef[4] = wet * mix_vertical
-    coef[5] = wet * (1.0 - 4.0 * mix_horizontal - 2.0 * mix_vertical)
-    coef[6] = wet
-
-    for t in range(TRIPLES):
-        ks = range(3 * t, min(3 * t + 3, K))
-        for lev in range(OL):
-            if lev == 0:
-                halo = [[lr[side, k * HW:(k + 1) * HW, :] for k in ks] for side in range(2)]
-                outer = edges(ls, lc, t)
-            else:
-                rows = [(k // 4) * 48 + (lev - 1) * 16 + (k % 4) * HW for k in ks]
-                halo = [[er[side, row:row + HW, :] for row in rows] for side in range(2)]
-                outer = edges(es, ec, t * 3 + lev - 1)
-            inner = widen([oc[k, lev] for k in ks], *halo) * coef[6, 0:BLK, :]
-            outer = outer * coef[6, BLK:COLS, :]
-            state[t, lev, 0:8, :] = outer
-            state[t, lev, 8:8 + BLK, :] = inner
-            state[t, lev, 8 + BLK:8 + COLS, :] = outer
-            state[t, lev, 8 + COLS:PADDED, :] = inner[0:8]
 
     def ocean(t, carry):
         for sub in range(NSUB):
@@ -540,8 +557,6 @@
         scratch_shapes=[
             pltpu.VMEM((K, LA, ACB * BLK), F32),
             pltpu.VMEM((3 * TRIPLES, OL, OY, BLK), F32),
-            pltpu.VMEM((7, COLS, BLK), F32),
-            pltpu.VMEM((TRIPLES, OL, PADDED, BLK), F32),
             pltpu.VMEM((2, OL, PADDED, BLK), F32),
             pltpu.SemaphoreType.DMA((K,)),
             pltpu.SemaphoreType.DMA((TRIPLES,)),

time: 34.8 us -> 32.4 us (0.931)
  Pallas kernels: 34.1 us -> 31.6 us
    pallas_call x1, Pallas kernels: 27.4 us -> 25.6 us  [exchange(): pl.pallas_call(exchange_kernel, out_shape=[jax.ShapeDtypeStruct(s, F32) f...]
    pallas_call x1, Pallas kernels: 6.67 us -> 5.99 us  [local_step(): pl.pallas_call(step_kernel, out_shape=[jax.ShapeDtypeStruct((K, LA, ACB *...]
where the time goes in v4:
time: 32.4 us; the launch traced here: 32.2 us
  Pallas kernels  31.6 us (98%)
  between operations  0.64 us (2%)
    pallas_call x1, Pallas kernels, exchange(): pl.pallas_call(exchange_kernel, out_shape=[jax.ShapeDtypeStruct(s, F32) f...  25.6 us
    pallas_call x1, Pallas kernels, local_step(): pl.pallas_call(step_kernel, out_shape=[jax.ShapeDtypeStruct((K, LA, ACB *...  5.99 us

profile of v4, /device:TPU:1, one launch (start us, length us, event | category | flops | bytes accessed | tf_op | source)
XLA Modules:
  0.0 32.2 jit_solution(13956408162454955432)
XLA Ops:
  0.6 25.6 %exchange.1 = (f32[16,72,1024]{2,1,0:T(8,128)S(1)}, f32[8,72,128]{2,1,0:T(8,128)S(1)}, f32[128,128]{1,0:T(8,128)S(1)}, f32[7,136,128]{2,1,0:T(8,128)S(1)}, f32[6,4,152,128]{3,2,1,0:T(8,128)S(1)}) custom-call(s32[3,72]{1,0:T(4,128)} %inter_hbm.1, f32[16,72,1024]{2,1,0:T(8,128)} %atm_hbm.1, f32[8,72,72]{2,1,0:T(8,128)} %mix_hbm.1, f32[16,4,32,128]{3,2,1,0:T(8,128)} %oc_hbm.1, ...), custom_call_target="tpu_custom_call" | custom-call | tf_op jit(solution)/shard_map/exchange/pallas_call | solution.py:439
  26.3 6.0 %step.1 = (f32[16,72,1024]{2,1,0:T(8,128)}, f32[16,4,32,128]{3,2,1,0:T(8,128)}) custom-call(f32[16,72,1024]{2,1,0:T(8,128)S(1)} %get-tuple-element.7.mixed, f32[8,72,128]{2,1,0:T(8,128)S(1)} %get-tuple-element.8.first_column, f32[128,128]{1,0:T(8,128)S(1)} %get-tuple-element.9.bottom, f32[7,136,128]{2,1,0:T(8,128)S(1)} %get-tuple-element.10.coef, ...), custom_call_target="tpu_custom_call" | custom-call | tf_op jit(solution)/shard_map/step/pallas_call | solution.py:549

commit v5 on v4

--- a/solution.py
+++ b/solution.py
@@ -479,35 +479,56 @@
 
 def step_kernel(
     mixed, first_column, bottom, coef, state,
-    atm_out, oc_out, atm_stage, oc_stage, work, asem, osem,
+    atm_out, oc_out, atm_stage, oc_stage, work, shift, asem, osem,
 ):
-    def surface_part(k, carry):
-        surface = bottom[pl.ds(pl.multiple_of(k * ACB, ACB), ACB), :]
-        for b in range(ACB):
-            cols = slice(b * BLK, (b + 1) * BLK)
-            atm_stage[k, :, cols] = mixed[k, :, cols] + first_column[b] * surface[b:b + 1]
-        pltpu.make_async_copy(atm_stage.at[k], atm_out.at[k], asem.at[k]).start()
-        return carry
-
-    lax.fori_loop(0, K, surface_part, 0)
+    row = lax.broadcasted_iota(jnp.int32, (2 * BLK, 2 * BLK), 0) % BLK
+    col = lax.broadcasted_iota(jnp.int32, (2 * BLK, 2 * BLK), 1)
+    step = jnp.where(col < BLK, 1, BLK - 1)
+    shift[...] = (row == (col + step) % BLK).astype(F32).astype(BF16)
 
     def ocean(t, carry):
+        for n in range(3):
+            k = jnp.minimum(3 * t + n, K - 1)
+            surface = bottom[pl.ds(pl.multiple_of(k * ACB, ACB), ACB), :]
+            for b in range(ACB):
+                cols = slice(b * BLK, (b + 1) * BLK)
+                atm_stage[3 * t + n, :, cols] = (
+                    mixed[k, :, cols] + first_column[b] * surface[b:b + 1]
+                )
         for sub in range(NSUB):
             def source(lev, start):
                 if sub == 0:
                     return state[t, lev, start:start + 8, :]
                 return work[(sub - 1) % 2, lev, start:start + 8, :]
 
-            for tile in range(COLS // 8):
+            bottom_level = OL - 1
+            whole = jnp.concatenate(
+                [source(bottom_level, 8 + tile * 8) for tile in range(COLS // 8 + 1)], 0
+            )
+            moved = dot(jnp.concatenate(split2(whole), 1), shift[...])
+
+            for tile, levels in (
+                [(tile, range(bottom_level)) for tile in range(COLS // 8)]
+                + [(tile, [bottom_level]) for tile in range(COLS // 8)]
+            ):
                 start = 8 + tile * 8
                 c = [coef[n, tile * 8:tile * 8 + 8, :] for n in range(6)]
-                x = [source(lev, start) for lev in range(OL)]
-                for lev in range(OL):
+                x = {
+                    lev: source(lev, start)
+                    for lev in range(max(levels[0] - 1, 0), min(levels[-1] + 2, OL))
+                }
+                for lev in levels:
+                    if lev == bottom_level:
+                        north = moved[tile * 8:tile * 8 + 8, 0:BLK]
+                        south = moved[tile * 8:tile * 8 + 8, BLK:2 * BLK]
+                    else:
+                        north = pltpu.roll(x[lev], BLK - 1, 1)
+                        south = pltpu.roll(x[lev], 1, 1)
                     new = (
                         c[0] * source(lev, start + 1)
                         + c[1] * source(lev, start - 1)
-                        + c[2] * pltpu.roll(x[lev], BLK - 1, 1)
-                        + c[3] * pltpu.roll(x[lev], 1, 1)
+                        + c[2] * north
+                        + c[3] * south
                         + c[4] * (x[max(lev - 1, 0)] + x[min(lev + 1, OL - 1)])
                         + c[5] * x[lev]
                     )
@@ -523,24 +544,26 @@
 
         @pl.when(t < TRIPLES - 1)
         def _():
-            pltpu.make_async_copy(
-                oc_stage.at[pl.ds(3 * t, 3)], oc_out.at[pl.ds(3 * t, 3)], osem.at[t]
-            ).start()
+            three = pl.ds(3 * t, 3)
+            pltpu.make_async_copy(atm_stage.at[three], atm_out.at[three], asem.at[t]).start()
+            pltpu.make_async_copy(oc_stage.at[three], oc_out.at[three], osem.at[t]).start()
 
         return carry
 
     lax.fori_loop(0, TRIPLES, ocean, 0)
-    last = pltpu.make_async_copy(
-        oc_stage.at[pl.ds(K - 1, 1)], oc_out.at[pl.ds(K - 1, 1)], osem.at[TRIPLES - 1]
-    )
-    last.start()
-    for k in range(K):
-        pltpu.make_async_copy(atm_stage.at[k], atm_out.at[k], asem.at[k]).wait()
+    copies = [
+        pltpu.make_async_copy(stage.at[part], out.at[part], sem.at[TRIPLES - 1])
+        for part in [pl.ds(K - 1, 1)]
+        for stage, out, sem in ((atm_stage, atm_out, asem), (oc_stage, oc_out, osem))
+    ]
+    for copy in copies:
+        copy.start()
     for t in range(TRIPLES - 1):
-        pltpu.make_async_copy(
-            oc_stage.at[pl.ds(3 * t, 3)], oc_out.at[pl.ds(3 * t, 3)], osem.at[t]
-        ).wait()
-    last.wait()
+        three = pl.ds(3 * t, 3)
+        pltpu.make_async_copy(atm_stage.at[three], atm_out.at[three], asem.at[t]).wait()
+        pltpu.make_async_copy(oc_stage.at[three], oc_out.at[three], osem.at[t]).wait()
+    for copy in copies:
+        copy.wait()
 
 
 def local_step(arrays):
@@ -555,10 +578,11 @@
         in_specs=[vmem] * len(arrays),
         out_specs=[hbm, hbm],
         scratch_shapes=[
-            pltpu.VMEM((K, LA, ACB * BLK), F32),
+            pltpu.VMEM((3 * TRIPLES, LA, ACB * BLK), F32),
             pltpu.VMEM((3 * TRIPLES, OL, OY, BLK), F32),
             pltpu.VMEM((2, OL, PADDED, BLK), F32),
-            pltpu.SemaphoreType.DMA((K,)),
+            pltpu.VMEM((2 * BLK, 2 * BLK), BF16),
+            pltpu.SemaphoreType.DMA((TRIPLES,)),
             pltpu.SemaphoreType.DMA((TRIPLES,)),
         ],
         compiler_params=pltpu.CompilerParams(vmem_limit_bytes=20 * 2**20),

time: 32.4 us -> 32.1 us (level)
  no operation moved by 1% of the time
where the time goes in v5:
time: 32.1 us; the launch traced here: 32 us
  Pallas kernels  31.3 us (98%)
  between operations  0.64 us (2%)
    pallas_call x1, Pallas kernels, exchange(): pl.pallas_call(exchange_kernel, out_shape=[jax.ShapeDtypeStruct(s, F32) f...  25.6 us
    pallas_call x1, Pallas kernels, local_step(): pl.pallas_call(step_kernel, out_shape=[jax.ShapeDtypeStruct((K, LA, ACB *...  5.7 us

profile of v5, /device:TPU:1, one launch (start us, length us, event | category | flops | bytes accessed | tf_op | source)
XLA Modules:
  0.0 32.0 jit_solution(9143564179714564919)
XLA Ops:
  0.6 25.6 %exchange.1 = (f32[16,72,1024]{2,1,0:T(8,128)S(1)}, f32[8,72,128]{2,1,0:T(8,128)S(1)}, f32[128,128]{1,0:T(8,128)S(1)}, f32[7,136,128]{2,1,0:T(8,128)S(1)}, f32[6,4,152,128]{3,2,1,0:T(8,128)S(1)}) custom-call(s32[3,72]{1,0:T(4,128)} %inter_hbm.1, f32[16,72,1024]{2,1,0:T(8,128)} %atm_hbm.1, f32[8,72,72]{2,1,0:T(8,128)} %mix_hbm.1, f32[16,4,32,128]{3,2,1,0:T(8,128)} %oc_hbm.1, ...), custom_call_target="tpu_custom_call" | custom-call | tf_op jit(solution)/shard_map/exchange/pallas_call | solution.py:439
  26.3 5.7 %step.1 = (f32[16,72,1024]{2,1,0:T(8,128)}, f32[16,4,32,128]{3,2,1,0:T(8,128)}) custom-call(f32[16,72,1024]{2,1,0:T(8,128)S(1)} %get-tuple-element.7.mixed, f32[8,72,128]{2,1,0:T(8,128)S(1)} %get-tuple-element.8.first_column, f32[128,128]{1,0:T(8,128)S(1)} %get-tuple-element.9.bottom, f32[7,136,128]{2,1,0:T(8,128)S(1)} %get-tuple-element.10.coef, ...), custom_call_target="tpu_custom_call" | custom-call | tf_op jit(solution)/shard_map/step/pallas_call | solution.py:572

commit v6 on v5

--- a/solution.py
+++ b/solution.py
@@ -405,12 +405,7 @@
             acc[b, K:K + 8, :] = wets
         return carry
 
-    lax.fori_loop(0, 9, return_group, 0)
-    for b in range(ACB):
-        old = abuf[:, 0, b * BLK:(b + 1) * BLK]
-        bottom[pl.ds(b, K, stride=ACB), :] = old + air_uptake * (
-            acc[b, 0:K, :] - acc[b, K:K + 1, :] * old
-        )
+    lax.fori_loop(0, 7, return_group, 0)
 
     all_of(LATE, rsem, spans[LATE])
     for t in range(TRIPLES):
@@ -419,6 +414,13 @@
         store_tile(
             state, coef, t, 0, widen([oc[k, 0] for k in ks], norths, souths),
             outer_columns(ls_in, lc_in, t, lane),
+        )
+
+    lax.fori_loop(7, 9, return_group, 0)
+    for b in range(ACB):
+        old = abuf[:, 0, b * BLK:(b + 1) * BLK]
+        bottom[pl.ds(b, K, stride=ACB), :] = old + air_uptake * (
+            acc[b, 0:K, :] - acc[b, K:K + 1, :] * old
         )
 
     for kind in range(5):

time: 32.1 us -> 32.2 us (level)
  no operation moved by 1% of the time
where the time goes in v6:
time: 32.2 us; the launch traced here: 32.1 us
  Pallas kernels  31.5 us (98%)
  between operations  0.64 us (2%)
    pallas_call x1, Pallas kernels, exchange(): pl.pallas_call(exchange_kernel, out_shape=[jax.ShapeDtypeStruct(s, F32) f...  25.8 us
    pallas_call x1, Pallas kernels, local_step(): pl.pallas_call(step_kernel, out_shape=[jax.ShapeDtypeStruct((K, LA, ACB *...  5.7 us

profile of v6, /device:TPU:1, one launch (start us, length us, event | category | flops | bytes accessed | tf_op | source)
XLA Modules:
  0.0 32.1 jit_solution(12946374040929822135)
XLA Ops:
  0.6 25.8 %exchange.1 = (f32[16,72,1024]{2,1,0:T(8,128)S(1)}, f32[8,72,128]{2,1,0:T(8,128)S(1)}, f32[128,128]{1,0:T(8,128)S(1)}, f32[7,136,128]{2,1,0:T(8,128)S(1)}, f32[6,4,152,128]{3,2,1,0:T(8,128)S(1)}) custom-call(s32[3,72]{1,0:T(4,128)} %inter_hbm.1, f32[16,72,1024]{2,1,0:T(8,128)} %atm_hbm.1, f32[8,72,72]{2,1,0:T(8,128)} %mix_hbm.1, f32[16,4,32,128]{3,2,1,0:T(8,128)} %oc_hbm.1, ...), custom_call_target="tpu_custom_call" | custom-call | tf_op jit(solution)/shard_map/exchange/pallas_call | solution.py:441
  26.4 5.7 %step.1 = (f32[16,72,1024]{2,1,0:T(8,128)}, f32[16,4,32,128]{3,2,1,0:T(8,128)}) custom-call(f32[16,72,1024]{2,1,0:T(8,128)S(1)} %get-tuple-element.7.mixed, f32[8,72,128]{2,1,0:T(8,128)S(1)} %get-tuple-element.8.first_column, f32[128,128]{1,0:T(8,128)S(1)} %get-tuple-element.9.bottom, f32[7,136,128]{2,1,0:T(8,128)S(1)} %get-tuple-element.10.coef, ...), custom_call_target="tpu_custom_call" | custom-call | tf_op jit(solution)/shard_map/step/pallas_call | solution.py:574

commit v7 on v5

--- a/solution.py
+++ b/solution.py
@@ -505,12 +505,15 @@
             whole = jnp.concatenate(
                 [source(bottom_level, 8 + tile * 8) for tile in range(COLS // 8 + 1)], 0
             )
-            moved = dot(jnp.concatenate(split2(whole), 1), shift[...])
-
-            for tile, levels in (
+            shifted_by_product = sub % 2 == 1
+            if shifted_by_product:
+                moved = dot(jnp.concatenate(split2(whole), 1), shift[...])
+
+            order = (
                 [(tile, range(bottom_level)) for tile in range(COLS // 8)]
                 + [(tile, [bottom_level]) for tile in range(COLS // 8)]
-            ):
+            ) if shifted_by_product else [(tile, range(OL)) for tile in range(COLS // 8)]
+            for tile, levels in order:
                 start = 8 + tile * 8
                 c = [coef[n, tile * 8:tile * 8 + 8, :] for n in range(6)]
                 x = {
@@ -518,7 +521,7 @@
                     for lev in range(max(levels[0] - 1, 0), min(levels[-1] + 2, OL))
                 }
                 for lev in levels:
-                    if lev == bottom_level:
+                    if lev == bottom_level and shifted_by_product:
                         north = moved[tile * 8:tile * 8 + 8, 0:BLK]
                         south = moved[tile * 8:tile * 8 + 8, BLK:2 * BLK]
                     else:

time: 32.1 us -> 31.9 us (level)
  no operation moved by 1% of the time
where the time goes in v7:
time: 31.9 us; the launch traced here: 31.8 us
  Pallas kernels  31.2 us (98%)
  between operations  0.64 us (2%)
    pallas_call x1, Pallas kernels, exchange(): pl.pallas_call(exchange_kernel, out_shape=[jax.ShapeDtypeStruct(s, F32) f...  25.6 us
    pallas_call x1, Pallas kernels, local_step(): pl.pallas_call(step_kernel, out_shape=[jax.ShapeDtypeStruct((K, LA, ACB *...  5.55 us

profile of v7, /device:TPU:1, one launch (start us, length us, event | category | flops | bytes accessed | tf_op | source)
XLA Modules:
  0.0 31.8 jit_solution(13393913834624337407)
XLA Ops:
  0.6 25.6 %exchange.1 = (f32[16,72,1024]{2,1,0:T(8,128)S(1)}, f32[8,72,128]{2,1,0:T(8,128)S(1)}, f32[128,128]{1,0:T(8,128)S(1)}, f32[7,136,128]{2,1,0:T(8,128)S(1)}, f32[6,4,152,128]{3,2,1,0:T(8,128)S(1)}) custom-call(s32[3,72]{1,0:T(4,128)} %inter_hbm.1, f32[16,72,1024]{2,1,0:T(8,128)} %atm_hbm.1, f32[8,72,72]{2,1,0:T(8,128)} %mix_hbm.1, f32[16,4,32,128]{3,2,1,0:T(8,128)} %oc_hbm.1, ...), custom_call_target="tpu_custom_call" | custom-call | tf_op jit(solution)/shard_map/exchange/pallas_call | solution.py:439
  26.3 5.5 %step.1 = (f32[16,72,1024]{2,1,0:T(8,128)}, f32[16,4,32,128]{3,2,1,0:T(8,128)}) custom-call(f32[16,72,1024]{2,1,0:T(8,128)S(1)} %get-tuple-element.7.mixed, f32[8,72,128]{2,1,0:T(8,128)S(1)} %get-tuple-element.8.first_column, f32[128,128]{1,0:T(8,128)S(1)} %get-tuple-element.9.bottom, f32[7,136,128]{2,1,0:T(8,128)S(1)} %get-tuple-element.10.coef, ...), custom_call_target="tpu_custom_call" | custom-call | tf_op jit(solution)/shard_map/step/pallas_call | solution.py:575
